TPU v7x, 128 devices: a whole 4x4x4 slice. The times are simulated.
128 devices in a mesh: dom: 16 (over y, x), slab: 8 (over z, core).
Axes of the slice: x: 4, y: 4, z: 4, core: 2. Of those that a mesh axis runs over, the one named last changes fastest.
Arguments:
- particles: bfloat16 [8192, 320, 256], P('dom', 'slab'), may hold values from -8 to 8
- blocks: int32 [8192, 2], P('dom'), may hold values from 0 to 3, as said below
- references: bfloat16 [512, 320, 256], P(None, 'slab'), may hold values from -1 to 1
- inv_noise: float32 [320], P('slab'), may hold values from 0.5 to 2
- destination: int32 [320, 512], replicated, may hold values from 0 to 127, as said below
- row_index: int32 [320, 512], replicated, may hold values from 0 to 254
- fraction: float32 [320, 512], replicated, may hold values from 0 to 1
Outputs:
- volume_data: float32 [32768, 256], P(('dom', 'slab'))
- next_slab: bfloat16 [4096, 2048], P(None, 'slab')
Inputs may be any that keep to these rules, and one draw needn't show every extreme that they name: Each particle names 2 different orientation blocks. destination is a device index in the order of the joined axes (dom, slab), dom major. Among the pieces whose group belongs to one index of slab and whose orientation belongs to one index of dom, no destination is named more than 16 times, and some destination exactly 16 times.
All inputs are finite; a program needn't handle non-finite values.
Results may differ from a plain program's by a relative error of at most 0.013.
Values may be sent and summed in bfloat16 or wider, within the bound.
A program may use at most 256 MiB of HBM per device.

v0:
```python
import jax
import jax.numpy as jnp
from jax import lax
from jax.sharding import PartitionSpec as P

OB = 128
RD = 256


def spread_rows(volume_rows, targets, fractions, values):
    lower_part = (1.0 - fractions)[:, None] * values
    upper_part = fractions[:, None] * values
    return volume_rows.at[targets].add(lower_part).at[targets + 1].add(upper_part)


def shards(particles, blocks, references, inv_noise, destination, row_index, fraction):
    particle_count, groups, row_width = particles.shape
    orients = references.shape[0]
    dom_size = lax.axis_size("dom")
    slab_size = lax.axis_size("slab")
    devices = dom_size * slab_size
    slab_pos = lax.axis_index("slab")
    weighted = (references.astype(jnp.float32) * inv_noise[None, :, None]).astype(jnp.bfloat16)
    weighted = weighted.reshape(orients, groups * row_width)
    flat_rows = particles.reshape(particle_count, groups * row_width)
    partial_value = lax.dot_general(
        flat_rows, weighted, (((1,), (1,)), ((), ())), preferred_element_type=jnp.float32
    )
    scores = lax.psum(partial_value, "slab")
    block_of = jnp.arange(orients, dtype=jnp.int32) // OB
    allowed = jnp.any(blocks[:, :, None] == block_of[None, None, :], axis=1)
    masked = jnp.where(allowed, scores, -jnp.inf)
    highest = jnp.max(masked, axis=1, keepdims=True)
    weights = jnp.where(allowed, jnp.exp(masked - highest), 0.0)
    posterior = (weights / jnp.sum(weights, axis=1, keepdims=True)).astype(jnp.bfloat16)
    slices = lax.dot_general(
        posterior, flat_rows, (((0,), (0,)), ((), ())), preferred_element_type=jnp.float32
    )
    slices = slices.astype(jnp.bfloat16).reshape(orients, groups, row_width)
    my_dest = lax.dynamic_slice_in_dim(destination, slab_pos * groups, groups, 0).T
    my_rows = lax.dynamic_slice_in_dim(row_index, slab_pos * groups, groups, 0).T
    my_frac = lax.dynamic_slice_in_dim(fraction, slab_pos * groups, groups, 0).T
    targets = (my_dest * RD + my_rows).reshape(-1)
    whole = jnp.zeros((RD * devices + 1, row_width), jnp.float32)
    whole = spread_rows(whole, targets, my_frac.reshape(-1), slices.reshape(-1, row_width))[
        : RD * devices
    ]
    volume = lax.psum_scatter(whole, ("dom", "slab"), scatter_dimension=0, tiled=True)
    next_slab = lax.all_gather(volume.astype(jnp.bfloat16), "dom", axis=0, tiled=True)
    return (volume, next_slab)


def solution(mesh):
    return jax.shard_map(
        shards,
        mesh=mesh,
        in_specs=(
            P("dom", "slab", None),
            P("dom", None),
            P(None, "slab", None),
            P("slab"),
            P(),
            P(),
            P(),
        ),
        out_specs=(P(("dom", "slab"), None), P(None, "slab")),
        check_vma=False,
    )
```

profile of v0, /device:TPU:0, one launch (start us, length us, event | category | flops | bytes accessed | tf_op | source)
XLA Modules:
  0.0 1183.2 jit_solution(17822718429548061716)
XLA Ops:
  7.2 0.0 copy-start
  7.2 0.0 all-reduce.2.cloned.1.call-start
  7.2 10.6 multiply_convert_fusion
  17.8 0.0 copy-start.2
  17.8 16.8 %fusion.11 = f32[512,512]{0,1:T(8,128)} fusion(bf16[512,40,256]{2,1,0:T(8,128)(2,1)} %param.7, bf16[512,40,256]{2,1,0:T(8,128)(2,1)} %multiply_convert_fusion), kind=kOutput, calls=%fused_computation.16 | convolution fusion | flops 5368709120 | bytes 22020096 | tf_op jit(solution)/shard_map/dot_general | solution.py:26
  34.6 0.0 all-reduce.2.cloned.1.call-update
  34.7 0.2 reduce-scatter.2.cloned.1.call-start
  34.9 0.0 copy-done
  34.9 0.1 copy.18
  35.1 0.2 reshape.93
  35.3 0.9 add_bitcast_fusion
  36.2 0.1 copy.17
  36.3 0.2 reshape.92
  36.6 0.2 compare_select_fusion
  36.8 0.0 copy-done.2
  36.8 0.2 compare_reduce_fusion
  37.0 0.3 copy.22
  37.4 11.6 copy.23
  49.0 51.2 %all-reduce.2.cloned.1.call-done = f32[512,512]{0,1:T(8,128)} async-done(((f32[512,512]{0,1:T(8,128)}), f32[512,512]{0,1:T(8,128)}) %all-reduce.2.cloned.1.call-update) | async-done | bytes 1048592 | tf_op jit(solution)/shard_map/psum | solution.py:29
  100.2 1.4 fusion.20
  101.6 1.5 fusion.16
  103.1 13.0 %fusion.5 = f32[512,10240]{1,0:T(8,128)} fusion(bf16[512,10240]{1,0:T(8,128)(2,1)} %bitcast.13, pred[512,512]{0,1:T(32,128)(4,1)S(1)} %copy.22, f32[512]{0:T(512)S(1)} %fusion.16, f32[512]{0:T(512)S(1)} %fusion.20, f32[512,512]{0,1:T(8,128)} %all-reduce.2.cloned.1.call-done), kind=kOutput, calls=%fused_computation.9 | convolution fusion | flops 5380505600 | bytes 32772096 | tf_op jit(solution)/shard_map/dot_general | solution.py:36
  116.1 20.6 %reshape.95 = f32[20480,256]{1,0:T(8,128)} reshape(f32[512,10240]{1,0:T(8,128)} %fusion.5) | data formatting | bytes 41943040 | tf_op jit(solution)/shard_map/convert_element_type | solution.py:11
  136.7 133.6 %scatter_custom_fusion = f32[32769,256]{1,0:T(8,128)} fusion(s32[20480]{0:T(1024)S(1)} %bitcast.16, f32[20480,256]{1,0:T(8,128)} %reshape.95, f32[]{:T(128)} %constant.15.clone.1, f32[20480]{0:T(1024)S(1)} %broadcast_subtract_fusion), kind=kCustom, calls=%fused_computation.4 | custom fusion | flops 10485760 | bytes 54608900 | tf_op jit(solution)/shard_map/scatter-add | solution.py:13
  270.3 142.0 %scatter_custom_fusion.1 = f32[32769,256]{1,0:T(8,128)} fusion(f32[32769,256]{1,0:T(8,128)} %scatter_custom_fusion, s32[20480]{0:T(1024)S(1)} %bitcast.15, f32[20480,256]{1,0:T(8,128)} %reshape.95, f32[20480]{0:T(1024)S(1)} %reshape.93), kind=kCustom, calls=%fused_computation.2 | custom fusion | flops 10485760 | bytes 54608896 | tf_op jit(solution)/shard_map/scatter-add | solution.py:13
  412.3 0.0 copy-start.1
  412.3 22.3 %slice.4 = f32[32768,256]{1,0:T(8,128)} slice(f32[32769,256]{1,0:T(8,128)} %scatter_custom_fusion.1), slice={[0:32768], [0:256]} | slice | bytes 67108864 | tf_op jit(solution)/shard_map/slice | solution.py:45
  434.6 0.0 reduce-scatter.2.cloned.1.call-update
  434.6 0.0 all-gather.2.cloned.1.call-start
  434.7 698.1 %reduce-scatter.2.cloned.1.call-done = f32[256,256]{1,0:T(8,128)} async-done(((f32[32768,256]{1,0:T(8,128)}), f32[256,256]{1,0:T(8,128)}) %reduce-scatter.2.cloned.1.call-update) | async-done | bytes 262160 | tf_op jit(solution)/shard_map/reduce_scatter | solution.py:48
  1132.8 1.6 convert_element_type.28
  1134.4 0.0 all-gather.2.cloned.1.call-update
  1134.4 39.2 %all-gather.2.cloned.1.call-done = bf16[4096,256]{1,0:T(8,128)(2,1)} async-done(((bf16[256,256]{1,0:T(8,128)(2,1)}), bf16[4096,256]{1,0:T(8,128)(2,1)}) %all-gather.2.cloned.1.call-update) | async-done | bytes 2097168 | tf_op jit(solution)/shard_map/all_gather | solution.py:49
  1173.6 3.0 copy.38
  1176.7 0.0 copy-done.1
  (3 shorter events, 0.0 us)
Async XLA Ops:
  7.2 27.8 %copy-start = (f32[320,512]{1,0:T(8,128)S(1)}, f32[320,512]{1,0:T(8,128)}, u32[]{:S(2)}) copy-start(f32[320,512]{1,0:T(8,128)} %param.13) | copy-start | bytes 1966084
  7.2 93.0 %all-reduce.2.cloned.1.call-start = ((), (), s32[]{:S(2)}) async-start(), calls=%async_computation.1 | async-start | bytes 2097152 | tf_op jit(solution)/shard_map/psum | solution.py:29
  17.8 18.9 %copy-start.2 = (s32[512,2]{0,1:T(2,128)S(1)}, s32[512,2]{0,1:T(2,128)}, u32[]{:S(2)}) copy-start(s32[512,2]{0,1:T(2,128)} %param.8) | copy-start | bytes 12292
  34.7 1098.1 %reduce-scatter.2.cloned.1.call-start = ((), (), s32[]{:S(2)}) async-start(), calls=%async_computation.2 | async-start | bytes 33816576 | tf_op jit(solution)/shard_map/reduce_scatter | solution.py:48
  412.3 764.4 %copy-start.1 = (f32[320,512]{1,0:T(8,128)S(1)}, f32[320,512]{1,0:T(8,128)}, u32[]{:S(2)}) copy-start(f32[320,512]{1,0:T(8,128)} %param.13) | copy-start | bytes 1966084
  434.6 739.0 %all-gather.2.cloned.1.call-start = ((), (), s32[]{:S(2)}) async-start(), calls=%async_computation.3 | async-start | bytes 2228224 | tf_op jit(solution)/shard_map/all_gather | solution.py:49
Sparse Core Ops, SparseCore 0:
  34.8 65.3 all-reduce.1
  434.8 697.9 reduce-scatter.1
  1135.5 38.0 all-gather.1
where the time goes:
time: 1180 us
  waiting for transfers between devices  789 us (67%)
  other arithmetic  292 us (25%)
  local copies, waits for them, and re-layouts  58.6 us (5%)
  matrix products  29.8 us (3%)
  between operations  13.9 us (1%)
    reduce_scatter x1, waiting for transfers between devices, shards(): lax.psum_scatter(whole, ('dom', 'slab'), scatter_dimension=0, tiled=True)  698 us
    scatter-add x2, other arithmetic, spread_rows(): volume_rows.at[targets].add(lower_part).at[targets + 1].add(upper_part)  276 us
    psum x1, waiting for transfers between devices, shards(): scores = lax.psum(partial_value, 'slab')  51.2 us
    all_gather x1, waiting for transfers between devices, shards(): lax.all_gather(volume.astype(jnp.bfloat16), 'dom', axis=0, tiled=True)  39.2 us
  transfers between devices with their start and end apart: 3, of which 3 were waited for; matrix products, arithmetic and copies ran while one was open for 1% of the time, Pallas kernels for 0%

commit v1 on v0

v1 whole, which is shorter than its diff:
```python
import jax
import jax.numpy as jnp
from jax import lax
from jax.sharding import PartitionSpec as P

OB = 128
RD = 256
CAP = 16


def send_slots(dests, devices):
    count = dests.shape[0]
    onehot = dests[:, None] == jnp.arange(devices, dtype=jnp.int32)[None, :]
    place = jnp.arange(count, dtype=jnp.int32)
    before = (place[None, :] < place[:, None]).astype(jnp.bfloat16)
    counts = jnp.dot(before, onehot.astype(jnp.bfloat16), preferred_element_type=jnp.float32)
    rank = jnp.sum(jnp.where(onehot, counts, 0.0), axis=1).astype(jnp.int32)
    return dests * CAP + rank


def received_slots(tables, dests, me):
    count = dests.shape[1]
    mask = dests == me
    place = jnp.arange(count, dtype=jnp.int32)
    before = (place[:, None] < place[None, :]).astype(jnp.bfloat16)
    rank = jnp.dot(mask.astype(jnp.bfloat16), before, preferred_element_type=jnp.float32)
    rank = jnp.where(mask, rank.astype(jnp.int32), -1)
    chosen = rank[:, None, :] == jnp.arange(CAP, dtype=jnp.int32)[None, :, None]
    found = [jnp.sum(jnp.where(chosen, t[:, None, :], 0), axis=2).reshape(-1) for t in tables]
    filled = jnp.any(chosen, axis=2).reshape(-1)
    return found, filled


def shards(particles, blocks, references, inv_noise, destination, row_index, fraction):
    particle_count, groups, row_width = particles.shape
    orients = references.shape[0]
    dom_size = lax.axis_size("dom")
    slab_size = lax.axis_size("slab")
    devices = dom_size * slab_size
    dom_pos = lax.axis_index("dom")
    slab_pos = lax.axis_index("slab")
    me = dom_pos * slab_size + slab_pos
    share = orients // dom_size
    weighted = (references.astype(jnp.float32) * inv_noise[None, :, None]).astype(jnp.bfloat16)
    partial_value = lax.dot_general(
        particles, weighted, (((1, 2), (1, 2)), ((), ())), preferred_element_type=jnp.float32
    )
    scores = lax.psum(partial_value, "slab")
    block_of = jnp.arange(orients, dtype=jnp.int32) // OB
    allowed = jnp.any(blocks[:, :, None] == block_of[None, None, :], axis=1)
    masked = jnp.where(allowed, scores, -jnp.inf)
    highest = jnp.max(masked, axis=1, keepdims=True)
    weights = jnp.where(allowed, jnp.exp(masked - highest), 0.0)
    posterior = (weights / jnp.sum(weights, axis=1, keepdims=True)).astype(jnp.bfloat16)
    slices = lax.dot_general(
        posterior,
        particles.reshape(particle_count, groups * row_width),
        (((0,), (0,)), ((), ())),
        preferred_element_type=jnp.float32,
    ).astype(jnp.bfloat16)
    mine = lax.psum_scatter(slices, "dom", scatter_dimension=0, tiled=True)
    pieces = mine.reshape(share * groups, row_width)

    my_dest = lax.dynamic_slice(
        destination, (slab_pos * groups, dom_pos * share), (groups, share)
    )
    slot = send_slots(my_dest.T.reshape(-1), devices)
    pack = jnp.arange(devices * CAP, dtype=jnp.int32)[:, None] == slot[None, :]
    packed = jnp.dot(
        pack.astype(jnp.bfloat16), pieces, preferred_element_type=jnp.float32
    ).astype(jnp.bfloat16)

    def by_source(table):
        table = table.reshape(slab_size, groups, dom_size, share).transpose(2, 0, 3, 1)
        return table.reshape(devices, share * groups)

    (row, part), filled = received_slots(
        (by_source(row_index), by_source(fraction)), by_source(destination), me
    )
    row = jnp.where(filled, row, -2)
    rows = jnp.arange(RD, dtype=jnp.int32)[:, None]
    insert = jnp.where(row[None, :] == rows, 1.0 - part[None, :], 0.0)
    insert = insert + jnp.where(row[None, :] + 1 == rows, part[None, :], 0.0)
    insert_high = insert.astype(jnp.bfloat16)
    insert_low = (insert - insert_high.astype(jnp.float32)).astype(jnp.bfloat16)

    got = lax.all_to_all(
        packed.reshape(devices, CAP, row_width), ("dom", "slab"), 0, 0, tiled=True
    ).reshape(devices * CAP, row_width)
    volume = jnp.dot(insert_high, got, preferred_element_type=jnp.float32)
    volume = volume + jnp.dot(insert_low, got, preferred_element_type=jnp.float32)
    next_slab = lax.all_gather(volume.astype(jnp.bfloat16), "dom", axis=0, tiled=True)
    return (volume, next_slab)


def solution(mesh):
    return jax.shard_map(
        shards,
        mesh=mesh,
        in_specs=(
            P("dom", "slab", None),
            P("dom", None),
            P(None, "slab", None),
            P("slab"),
            P(),
            P(),
            P(),
        ),
        out_specs=(P(("dom", "slab"), None), P(None, "slab")),
        check_vma=False,
    )
```

time: 1180 us -> 288 us (0.24)
  waiting for transfers between devices: 789 us -> 178 us
  other arithmetic: 292 us -> 19.5 us
  local copies, waits for them, and re-layouts: 58.6 us -> 32.8 us
    reduce_scatter x1, waiting for transfers between devices: 698 us -> 67.8 us  [shards(): mine = lax.psum_scatter(slices, 'dom', scatter_dimension=0, tiled=True)]
    scatter-add x2 -> x0, other arithmetic: 276 us -> none  [spread_rows(): volume_rows.at[targets].add(lower_part).at[targets + 1].add(upper_part)]
    slice x1 -> x0, local copies, waits for them, and re-layouts: 22.3 us -> none  [shards(): spread_rows(whole, targets, my_frac.reshape(-1), slices.reshape(-1, row_w...]
    convert_element_type x1 -> x0, local copies, waits for them, and re-layouts: 20.6 us -> none  [spread_rows(): lower_part = (1.0 - fractions)[:, None] * values]
    all_to_all x0 -> x1, waiting for transfers between devices: none -> 16.8 us  [shards(): lax.all_to_all(packed.reshape(devices, CAP, row_width), ('dom', 'slab'),...]
    dot_general x2 -> x7, matrix products: 29.8 us -> 34.1 us  [the longest x1 16.8 us: shards(): lax.dot_general(particles, weighted, (((1, 2), (1, 2)), ((), ())), prefer...]
  transfers between devices with their start and end apart: 3 -> 4, of which waited for: 3 -> 4; matrix products, arithmetic and copies ran while one was open for 1% -> 12% of each run, Pallas kernels for 0% -> 0%
where the time goes in v1:
time: 288 us; the launch traced here: 287 us
  waiting for transfers between devices  178 us (62%)
  matrix products  34.1 us (12%)
  local copies, waits for them, and re-layouts  32.8 us (11%)
  other arithmetic  19.5 us (7%)
  between operations  13.9 us (5%)
  starting transfers between devices  8.31 us (3%)
    reduce_scatter x1, waiting for transfers between devices, shards(): mine = lax.psum_scatter(slices, 'dom', scatter_dimension=0, tiled=True)  67.8 us
    psum x1, waiting for transfers between devices, shards(): scores = lax.psum(partial_value, 'slab')  53.2 us
    all_gather x1, waiting for transfers between devices, shards(): lax.all_gather(volume.astype(jnp.bfloat16), 'dom', axis=0, tiled=True)  40.5 us
    unnamed x10, local copies, waits for them, and re-layouts  17.2 us
    all_to_all x1, waiting for transfers between devices, shards(): lax.all_to_all(packed.reshape(devices, CAP, row_width), ('dom', 'slab'),...  16.8 us
    dot_general x1, matrix products, shards(): lax.dot_general(particles, weighted, (((1, 2), (1, 2)), ((), ())), prefer...  16.8 us
    dot_general x1, matrix products, shards(): lax.dot_general(posterior, particles.reshape(particle_count, groups * row...  11 us
    convert_element_type x1, other arithmetic, shards(): (references.astype(jnp.float32) * inv_noise[None, :, None]).astype(jnp.bf...  10.6 us
  transfers between devices with their start and end apart: 4, of which 4 were waited for; matrix products, arithmetic and copies ran while one was open for 12% of the time, Pallas kernels for 0%

profile of v1, /device:TPU:0, one launch (start us, length us, event | category | flops | bytes accessed | tf_op | source)
XLA Modules:
  0.0 287.1 jit_solution(18362799197810105035)
XLA Ops:
  7.2 0.0 all-reduce.2.cloned.1.call-start
  7.2 10.6 %multiply_convert_fusion = bf16[512,40,256]{2,1,0:T(8,128)(2,1)} fusion(bf16[512,40,256]{2,1,0:T(8,128)(2,1)} %param.9, f32[40]{0:T(128)} %param.10), kind=kLoop, calls=%fused_computation | loop fusion | flops 15728640 | bytes 20971680 | tf_op jit(solution)/shard_map/convert_element_type | solution.py:44
  17.8 16.8 %fusion.13 = f32[512,512]{0,1:T(8,128)} fusion(bf16[512,40,256]{2,1,0:T(8,128)(2,1)} %param.7, bf16[512,40,256]{2,1,0:T(8,128)(2,1)} %multiply_convert_fusion), kind=kOutput, calls=%fused_computation.26 | convolution fusion | flops 5368709120 | bytes 22020096 | tf_op jit(solution)/shard_map/dot_general | solution.py:45
  34.6 0.0 all-reduce.2.cloned.1.call-update
  34.6 0.2 reduce-scatter.2.cloned.1.call-start
  34.8 11.5 %copy.36 = bf16[64,8,40,256]{3,1,2,0:T(8,128)(2,1)} copy(bf16[64,8,40,256]{3,2,1,0:T(8,128)(2,1)} %bitcast.30) | data formatting | bytes 20971520
  46.3 0.2 compare_reduce_fusion
  46.5 0.3 copy.34
  46.9 53.2 %all-reduce.2.cloned.1.call-done = f32[512,512]{0,1:T(8,128)} async-done(((f32[512,512]{0,1:T(8,128)}), f32[512,512]{0,1:T(8,128)}) %all-reduce.2.cloned.1.call-update) | async-done | bytes 1048592 | tf_op jit(solution)/shard_map/psum | solution.py:48
  100.1 1.4 fusion.30
  101.5 1.5 fusion.26
  103.0 11.0 %convolution_convert_fusion = bf16[512,10240]{1,0:T(8,128)(2,1)} fusion(bf16[512,10240]{1,0:T(8,128)(2,1)} %bitcast.31, pred[512,512]{0,1:T(32,128)(4,1)S(1)} %copy.34, f32[512]{0:T(512)S(1)} %fusion.26, f32[512]{0:T(512)S(1)} %fusion.30, f32[512,512]{0,1:T(8,128)} %all-reduce.2.cloned.1.call-done), kind=kOutput, calls=%fused_computation.1 | convolution fusion | flops 5375262720 | bytes 22286336 | tf_op jit(solution)/shard_map/dot_general | solution.py:55
  114.0 0.0 reduce-scatter.2.cloned.1.call-update
  114.0 1.1 copy-done
  115.1 0.1 dynamic-slice_bitcast_fusion
  115.2 0.1 copy.29
  115.2 0.1 reshape.92
  115.3 0.3 copy.27
  115.6 0.8 reshape.91
  116.4 1.7 copy.28
  118.1 2.7 broadcast_in_dim.87
  120.8 0.1 broadcast_compare_fusion
  120.9 0.3 copy.23
  121.2 0.9 eq.95
  122.2 0.3 copy.24
  122.5 1.3 eq.97
  123.8 0.6 fusion.11
  124.4 1.1 select_reduce_fusion
  125.5 0.1 broadcast_in_dim_reshape.2
  125.6 1.4 copy.25
  127.0 0.8 reshape.90
  127.8 1.7 copy.26
  129.5 3.0 %broadcast_in_dim.83 = s32[128,1280]{1,0:T(8,128)S(1)} reshape(s32[16,8,32,40]{3,2,1,0:T(8,128)} %copy.26) | data formatting | bytes 1310720 | tf_op jit(solution)/shard_map/jit(_where)/broadcast_in_dim | solution.py:29
  132.4 0.9 fusion.18
  133.4 2.3 fusion.3
  135.6 67.8 %reduce-scatter.2.cloned.1.call-done = bf16[32,10240]{1,0:T(8,128)(2,1)} async-done(((bf16[512,10240]{1,0:T(8,128)(2,1)}), bf16[32,10240]{1,0:T(8,128)(2,1)}) %reduce-scatter.2.cloned.1.call-update) | async-done | bytes 655376 | tf_op jit(solution)/shard_map/reduce_scatter | solution.py:61
  203.5 1.4 reshape.94
  204.9 2.9 %fusion.8 = bf16[2048,256]{1,0:T(8,128)(2,1)} fusion(bf16[1280,256]{1,0:T(8,128)(2,1)S(1)} %reshape.94, s32[1280]{0:T(1024)S(1)} %convert_add_fusion), kind=kOutput, calls=%fused_computation.16 | convolution fusion | flops 1345323008 | bytes 1709056 | tf_op jit(solution)/shard_map/dot_general | solution.py:69
  207.8 8.0 %all-to-all-start = ((bf16[128,16,256]{2,1,0:T(8,128)(2,1)}), bf16[128,16,256]{2,1,0:T(8,128)(2,1)S(1)}, u32[]{:S(2)}, u32[]{:S(2)}) async-start(bf16[128,16,256]{2,1,0:T(8,128)(2,1)} %bitcast.37), calls=%async_computation.1 | async-start | bytes 2097152 | tf_op jit(solution)/shard_map/all_to_all | solution.py:87
  215.8 0.0 all-gather.2.cloned.1.call-start
  215.9 2.3 select_reduce_fusion.1
  218.1 0.1 select_n.62
  218.2 16.8 %all-to-all-done = bf16[128,16,256]{2,1,0:T(8,128)(2,1)S(1)} async-done(((bf16[128,16,256]{2,1,0:T(8,128)(2,1)}), bf16[128,16,256]{2,1,0:T(8,128)(2,1)S(1)}, u32[]{:S(2)}, u32[]{:S(2)}) %all-to-all-start) | async-done | bytes 1048608 | tf_op jit(solution)/shard_map/all_to_all | solution.py:87
  235.1 0.5 fusion.24
  235.6 1.4 fusion.39
  237.0 0.0 all-gather.2.cloned.1.call-update
  237.0 40.5 %all-gather.2.cloned.1.call-done = bf16[4096,256]{1,0:T(8,128)(2,1)} async-done(((bf16[256,256]{1,0:T(8,128)(2,1)}), bf16[4096,256]{1,0:T(8,128)(2,1)}) %all-gather.2.cloned.1.call-update) | async-done | bytes 2097168 | tf_op jit(solution)/shard_map/all_gather | solution.py:92
  277.5 3.0 %copy.52 = bf16[4096,256]{1,0:T(8,128)(2,1)} copy(bf16[4096,256]{1,0:T(8,128)(2,1)} %all-gather.2.cloned.1.call-done) | data formatting | bytes 4194304
  (10 shorter events, 0.0 us)
Async XLA Ops:
  7.2 92.9 %all-reduce.2.cloned.1.call-start = ((), (), s32[]{:S(2)}) async-start(), calls=%async_computation.2 | async-start | bytes 2097152 | tf_op jit(solution)/shard_map/psum | solution.py:48
  34.6 168.9 %reduce-scatter.2.cloned.1.call-start = ((), (), s32[]{:S(2)}) async-start(), calls=%async_computation.3 | async-start | bytes 11141120 | tf_op jit(solution)/shard_map/reduce_scatter | solution.py:61
  34.8 11.5 %copy-start.2 = (s32[512,2]{0,1:T(2,128)S(1)}, s32[512,2]{0,1:T(2,128)}, u32[]{:S(2)}) copy-start(s32[512,2]{0,1:T(2,128)} %param.8) | copy-start | bytes 12292
  114.0 1.1 copy-start
  114.0 1.3 copy-start.1
  207.8 27.3 %all-to-all-start = ((bf16[128,16,256]{2,1,0:T(8,128)(2,1)}), bf16[128,16,256]{2,1,0:T(8,128)(2,1)S(1)}, u32[]{:S(2)}, u32[]{:S(2)}) async-start(bf16[128,16,256]{2,1,0:T(8,128)(2,1)} %bitcast.37), calls=%async_computation.1 | async-start | bytes 2097152 | tf_op jit(solution)/shard_map/all_to_all | solution.py:87
  215.8 61.7 %all-gather.2.cloned.1.call-start = ((), (), s32[]{:S(2)}) async-start(), calls=%async_computation.4 | async-start | bytes 2228224 | tf_op jit(solution)/shard_map/all_gather | solution.py:92
Sparse Core Ops, SparseCore 0:
  34.7 65.3 all-reduce.1
  114.1 89.2 reduce-scatter.1
  237.1 40.3 all-gather.1

commit v2 on v1

--- a/solution.py
+++ b/solution.py
@@ -1,11 +1,181 @@
+import functools
+
 import jax
 import jax.numpy as jnp
 from jax import lax
+from jax.experimental import pallas as pl
+from jax.experimental.pallas import tpu as pltpu
 from jax.sharding import PartitionSpec as P
 
+MESH = pl.DeviceIdType.MESH
 OB = 128
 RD = 256
 CAP = 16
+SIDE = 4
+CHUNKS = 5
+ROUTES = (("x", 1), ("x", -1), ("y", 1), ("y", -1))
+
+
+class Torus:
+    def __init__(self):
+        dom = lax.axis_index("dom")
+        self.slab = lax.axis_index("slab")
+        self.at = {"y": lax.div(dom, SIDE), "x": lax.rem(dom, SIDE)}
+
+    def neighbour(self, axis, step):
+        at = dict(self.at)
+        at[axis] = lax.rem(at[axis] + step + SIDE, SIDE)
+        return (at["y"] * SIDE + at["x"], self.slab)
+
+
+def other(axis):
+    return "y" if axis == "x" else "x"
+
+
+def sum_kernel(x_ref, post_ref, out_ref, images, partial, got1, got2, in_sem, send1, recv1, send2, recv2):
+    torus = Torus()
+    per_chunk = x_ref.shape[0] // (len(ROUTES) * CHUNKS)
+    share = out_ref.shape[1]
+
+    def fetch(q, i):
+        first = (q * CHUNKS + i) * per_chunk
+        return pltpu.make_async_copy(
+            x_ref.at[pl.ds(first, per_chunk)], images.at[q, i], in_sem.at[q, i]
+        )
+
+    def block(q, stage, hop):
+        axis, sign = ROUTES[q]
+        axis = axis if stage == 1 else other(axis)
+        return lax.rem(torus.at[axis] - sign * (1 + hop) + 2 * SIDE, SIDE)
+
+    def hop1(q, hop, i):
+        axis, sign = ROUTES[q]
+        source = partial.at[q, i, block(q, 1, 0)] if hop == 0 else got1.at[q, hop - 1, i]
+        return pltpu.make_async_remote_copy(
+            src_ref=source,
+            dst_ref=got1.at[q, hop, i],
+            send_sem=send1.at[q, hop, i],
+            recv_sem=recv1.at[q, hop, i],
+            device_id=torus.neighbour(axis, sign),
+            device_id_type=MESH,
+        )
+
+    def hop2(q, hop, i):
+        axis, sign = ROUTES[q]
+        source = got1.at[q, SIDE - 2, i, block(q, 2, 0)] if hop == 0 else got2.at[q, hop - 1, i]
+        return pltpu.make_async_remote_copy(
+            src_ref=source,
+            dst_ref=got2.at[q, hop, i],
+            send_sem=send2.at[q, hop, i],
+            recv_sem=recv2.at[q, hop, i],
+            device_id=torus.neighbour(other(axis), sign),
+            device_id_type=MESH,
+        )
+
+    def added(a, b):
+        return (a.astype(jnp.float32) + b.astype(jnp.float32)).astype(jnp.bfloat16)
+
+    routes = range(len(ROUTES))
+    for i in range(CHUNKS):
+        for q in routes:
+            fetch(q, i).start()
+    barrier = pltpu.get_barrier_semaphore()
+    for axis, sign in ROUTES:
+        pl.semaphore_signal(
+            barrier, inc=1, device_id=torus.neighbour(axis, sign), device_id_type=MESH
+        )
+    pl.semaphore_wait(barrier, len(ROUTES))
+
+    @pl.loop(0, CHUNKS)
+    def _(i):
+        for q in routes:
+            fetch(q, i).wait()
+            for j in range(per_chunk):
+                value = jnp.dot(
+                    post_ref[...], images[q, i, j], preferred_element_type=jnp.float32
+                ).astype(jnp.bfloat16)
+                for yy in range(SIDE):
+                    for xx in range(SIDE):
+                        first, second = (xx, yy) if ROUTES[q][0] == "x" else (yy, xx)
+                        begin = (yy * SIDE + xx) * share
+                        partial[q, i, first, second, j] = value[begin : begin + share]
+            hop1(q, 0, i).start()
+
+    for hop in range(SIDE - 2):
+
+        @pl.loop(0, CHUNKS)
+        def _(i):
+            for q in routes:
+                hop1(q, hop, i).wait_recv()
+                got1[q, hop, i] = added(got1[q, hop, i], partial[q, i, block(q, 1, hop + 1)])
+                hop1(q, hop + 1, i).start()
+
+    last = SIDE - 2
+
+    @pl.loop(0, CHUNKS)
+    def _(i):
+        for q in routes:
+            hop1(q, last, i).wait_recv()
+            got1[q, last, i] = added(got1[q, last, i], partial[q, i, torus.at[ROUTES[q][0]]])
+            hop2(q, 0, i).start()
+
+    for hop in range(SIDE - 2):
+
+        @pl.loop(0, CHUNKS)
+        def _(i):
+            for q in routes:
+                hop2(q, hop, i).wait_recv()
+                got2[q, hop, i] = added(got2[q, hop, i], got1[q, last, i, block(q, 2, hop + 1)])
+                hop2(q, hop + 1, i).start()
+
+    @pl.loop(0, CHUNKS)
+    def _(i):
+        for q in routes:
+            hop2(q, last, i).wait_recv()
+            mine = got1[q, last, i, torus.at[other(ROUTES[q][0])]]
+            first = (q * CHUNKS + i) * per_chunk
+            out_ref[pl.ds(first, per_chunk)] = added(got2[q, last, i], mine)
+
+    @pl.loop(0, CHUNKS)
+    def _(i):
+        for q in routes:
+            for hop in range(SIDE - 1):
+                hop1(q, hop, i).wait_send()
+                hop2(q, hop, i).wait_send()
+
+
+def summed_slices(images, posterior, share):
+    groups, particles, width = images.shape
+    orients = posterior.shape[0]
+    routes = len(ROUTES)
+    per_chunk = groups // (routes * CHUNKS)
+    hops = SIDE - 1
+    piece = (per_chunk, share, width)
+    sems = pltpu.SemaphoreType.DMA((routes, hops, CHUNKS))
+    return pl.pallas_call(
+        sum_kernel,
+        out_shape=jax.ShapeDtypeStruct((groups, share, width), jnp.bfloat16),
+        in_specs=[
+            pl.BlockSpec(memory_space=pl.ANY),
+            pl.BlockSpec(memory_space=pltpu.VMEM),
+        ],
+        out_specs=pl.BlockSpec(memory_space=pltpu.VMEM),
+        scratch_shapes=[
+            pltpu.VMEM((routes, CHUNKS, per_chunk, particles, width), jnp.bfloat16),
+            pltpu.VMEM((routes, CHUNKS, SIDE, SIDE) + piece, jnp.bfloat16),
+            pltpu.VMEM((routes, hops, CHUNKS, SIDE) + piece, jnp.bfloat16),
+            pltpu.VMEM((routes, hops, CHUNKS) + piece, jnp.bfloat16),
+            pltpu.SemaphoreType.DMA((routes, CHUNKS)),
+            sems,
+            sems,
+            sems,
+            sems,
+        ],
+        compiler_params=pltpu.CompilerParams(
+            collective_id=0, has_side_effects=True, vmem_limit_bytes=48 * 1024 * 1024
+        ),
+        name="sum_slices",
+    )(images, posterior)
 
 
 def send_slots(dests, devices):
@@ -43,35 +213,29 @@
     share = orients // dom_size
     weighted = (references.astype(jnp.float32) * inv_noise[None, :, None]).astype(jnp.bfloat16)
     partial_value = lax.dot_general(
-        particles, weighted, (((1, 2), (1, 2)), ((), ())), preferred_element_type=jnp.float32
+        weighted, particles, (((1, 2), (1, 2)), ((), ())), preferred_element_type=jnp.float32
     )
     scores = lax.psum(partial_value, "slab")
     block_of = jnp.arange(orients, dtype=jnp.int32) // OB
-    allowed = jnp.any(blocks[:, :, None] == block_of[None, None, :], axis=1)
+    allowed = jnp.any(blocks.T[:, None, :] == block_of[None, :, None], axis=0)
     masked = jnp.where(allowed, scores, -jnp.inf)
-    highest = jnp.max(masked, axis=1, keepdims=True)
+    highest = jnp.max(masked, axis=0, keepdims=True)
     weights = jnp.where(allowed, jnp.exp(masked - highest), 0.0)
-    posterior = (weights / jnp.sum(weights, axis=1, keepdims=True)).astype(jnp.bfloat16)
-    slices = lax.dot_general(
-        posterior,
-        particles.reshape(particle_count, groups * row_width),
-        (((0,), (0,)), ((), ())),
-        preferred_element_type=jnp.float32,
-    ).astype(jnp.bfloat16)
-    mine = lax.psum_scatter(slices, "dom", scatter_dimension=0, tiled=True)
-    pieces = mine.reshape(share * groups, row_width)
+    posterior = (weights / jnp.sum(weights, axis=0, keepdims=True)).astype(jnp.bfloat16)
+    pieces = summed_slices(particles.transpose(1, 0, 2), posterior, share)
+    pieces = pieces.reshape(groups * share, row_width)
 
     my_dest = lax.dynamic_slice(
         destination, (slab_pos * groups, dom_pos * share), (groups, share)
     )
-    slot = send_slots(my_dest.T.reshape(-1), devices)
+    slot = send_slots(my_dest.reshape(-1), devices)
     pack = jnp.arange(devices * CAP, dtype=jnp.int32)[:, None] == slot[None, :]
     packed = jnp.dot(
         pack.astype(jnp.bfloat16), pieces, preferred_element_type=jnp.float32
     ).astype(jnp.bfloat16)
 
     def by_source(table):
-        table = table.reshape(slab_size, groups, dom_size, share).transpose(2, 0, 3, 1)
+        table = table.reshape(slab_size, groups, dom_size, share).transpose(2, 0, 1, 3)
         return table.reshape(devices, share * groups)
 
     (row, part), filled = received_slots(

time: 288 us -> 250 us (0.87)
  waiting for transfers between devices: 178 us -> 88.2 us
  Pallas kernels: 0 us -> 63.4 us
  matrix products: 34.1 us -> 25.7 us
  local copies, waits for them, and re-layouts: 32.8 us -> 29.7 us
    reduce_scatter x1 -> x0, waiting for transfers between devices: 67.8 us -> none  [shards(): mine = lax.psum_scatter(slices, 'dom', scatter_dimension=0, tiled=True)]
    pallas_call x0 -> x1, Pallas kernels: none -> 63.4 us  [summed_slices(): pl.pallas_call(sum_kernel, out_shape=jax.ShapeDtypeStruct((groups, share,...]
    psum x1, waiting for transfers between devices: 53.2 us -> 37.4 us  [shards(): scores = lax.psum(partial_value, 'slab')]
    dot_general x2 -> x1, matrix products: 27.8 us -> 16.8 us  [shards(): lax.dot_general(weighted, particles, (((1, 2), (1, 2)), ((), ())), prefer...]
    all_to_all x1, waiting for transfers between devices: 16.8 us -> 10.3 us  [shards(): lax.all_to_all(packed.reshape(devices, CAP, row_width), ('dom', 'slab'),...]
    unnamed x10 -> x14, local copies, waits for them, and re-layouts: 17.2 us -> 14.1 us
  transfers between devices with their start and end apart: 4 -> 3, of which waited for: 4 -> 3; matrix products, arithmetic and copies ran while one was open for 12% -> 15% of each run, Pallas kernels for 0% -> 0%
where the time goes in v2:
time: 250 us
  waiting for transfers between devices  88.2 us (35%)
  Pallas kernels  63.4 us (25%)
  local copies, waits for them, and re-layouts  29.7 us (12%)
  matrix products  25.7 us (10%)
  other arithmetic  22.1 us (9%)
  between operations  14.3 us (6%)
  starting transfers between devices  6.3 us (3%)
    pallas_call x1, Pallas kernels, summed_slices(): pl.pallas_call(sum_kernel, out_shape=jax.ShapeDtypeStruct((groups, share,...  63.4 us
    all_gather x1, waiting for transfers between devices, shards(): lax.all_gather(volume.astype(jnp.bfloat16), 'dom', axis=0, tiled=True)  40.5 us
    psum x1, waiting for transfers between devices, shards(): scores = lax.psum(partial_value, 'slab')  37.4 us
    dot_general x1, matrix products, shards(): lax.dot_general(weighted, particles, (((1, 2), (1, 2)), ((), ())), prefer...  16.8 us
    unnamed x14, local copies, waits for them, and re-layouts  14.1 us
    convert_element_type x1, other arithmetic, shards(): (references.astype(jnp.float32) * inv_noise[None, :, None]).astype(jnp.bf...  10.6 us
    all_to_all x1, waiting for transfers between devices, shards(): lax.all_to_all(packed.reshape(devices, CAP, row_width), ('dom', 'slab'),...  10.3 us
    all_to_all x1, starting transfers between devices, shards(): lax.all_to_all(packed.reshape(devices, CAP, row_width), ('dom', 'slab'),...  6.22 us
  transfers between devices with their start and end apart: 3, of which 3 were waited for; matrix products, arithmetic and copies ran while one was open for 15% of the time, Pallas kernels for 0%

profile of v2, /device:TPU:0, one launch (start us, length us, event | category | flops | bytes accessed | tf_op | source)
XLA Modules:
  0.0 249.6 jit_solution(15824705322509232680)
XLA Ops:
  7.2 0.0 all-reduce.2.cloned.1.call-start
  7.2 10.6 %multiply_convert_fusion = bf16[512,40,256]{2,1,0:T(8,128)(2,1)} fusion(bf16[512,40,256]{2,1,0:T(8,128)(2,1)} %param.9, f32[40]{0:T(128)} %param.10), kind=kLoop, calls=%fused_computation | loop fusion | flops 15728640 | bytes 20971680 | tf_op jit(solution)/shard_map/convert_element_type | solution.py:214
  17.8 16.8 %fusion.13 = f32[512,512]{1,0:T(8,128)} fusion(bf16[512,40,256]{2,1,0:T(8,128)(2,1)} %param.7, bf16[512,40,256]{2,1,0:T(8,128)(2,1)} %multiply_convert_fusion), kind=kOutput, calls=%fused_computation.26 | convolution fusion | flops 5368709120 | bytes 22020096 | tf_op jit(solution)/shard_map/dot_general | solution.py:215
  34.6 0.0 all-reduce.2.cloned.1.call-update
  34.6 0.0 copy-start.1
  34.6 10.5 %copy.42 = bf16[512,40,256]{2,0,1:T(8,128)(2,1)} copy(bf16[512,40,256]{2,1,0:T(8,128)(2,1)} %param.7) | data formatting | bytes 20971520 | tf_op args[0]
  45.1 0.0 copy-done.1
  45.1 0.1 dynamic_slice.3
  45.2 0.1 reshape.89
  45.3 0.9 fusion.18
  46.3 0.1 broadcast_compare_fusion
  46.3 0.3 copy.22
  46.7 0.9 eq.95
  47.6 0.0 copy-start.2
  47.6 1.4 copy.23
  49.1 1.1 eq.97
  50.2 0.6 fusion.11
  50.8 0.0 copy-done.2
  50.8 0.3 copy.24
  51.0 2.1 reshape.87
  53.2 2.1 copy.25
  55.3 0.0 copy-start.4
  55.3 1.5 broadcast_in_dim.83
  56.8 2.3 fusion.2
  59.1 0.0 copy-done.4
  59.1 0.2 compare_reduce_fusion
  59.3 3.3 %select_reduce_fusion.1 = s32[128,16]{1,0:T(8,128)S(1)} fusion(s32[128,1280]{1,0:T(8,128)} %broadcast_in_dim.83, s32[128,1280]{1,0:T(8,128)S(1)} %fusion.11), kind=kLoop, calls=%fused_computation.5 | loop fusion | flops 7862272 | bytes 1318912 | tf_op jit(solution)/shard_map/reduce_sum | solution.py:199
  62.7 37.4 %all-reduce.2.cloned.1.call-done = f32[512,512]{1,0:T(8,128)} async-done(((f32[512,512]{1,0:T(8,128)}), f32[512,512]{1,0:T(8,128)}) %all-reduce.2.cloned.1.call-update) | async-done | bytes 1048592 | tf_op jit(solution)/shard_map/psum | solution.py:218
  100.1 1.5 fusion.27
  101.6 1.5 fusion.26
  103.1 0.3 divide_convert_fusion.post_ref
  103.4 63.4 %sum_slices.1 = bf16[40,32,256]{2,1,0:T(8,128)(2,1)S(1)} custom-call(bf16[40,512,256]{2,1,0:T(8,128)(2,1)} %bitcast.29, bf16[512,512]{1,0:T(8,128)(2,1)S(1)} %divide_convert_fusion.post_ref), custom_call_target="tpu_custom_call" | custom-call | tf_op jit(solution)/shard_map/sum_slices/pallas_call | solution.py:155
  166.8 3.0 %fusion.8 = bf16[2048,256]{1,0:T(8,128)(2,1)} fusion(bf16[1280,256]{1,0:T(8,128)(2,1)S(1)} %bitcast.28, s32[1280]{0:T(1024)S(1)} %convert_add_fusion), kind=kOutput, calls=%fused_computation.16 | convolution fusion | flops 1345323008 | bytes 1709056 | tf_op jit(solution)/shard_map/dot_general | solution.py:233
  169.8 6.2 %all-to-all-start = ((bf16[128,16,256]{2,1,0:T(8,128)(2,1)}), bf16[128,16,256]{2,1,0:T(8,128)(2,1)}, u32[]{:S(2)}, u32[]{:S(2)}) async-start(bf16[128,16,256]{2,1,0:T(8,128)(2,1)} %bitcast.7), calls=%async_computation | async-start | bytes 2097152 | tf_op jit(solution)/shard_map/all_to_all | solution.py:251
  176.0 0.0 all-gather.2.cloned.1.call-start
  176.1 0.1 select_n.62
  176.2 0.3 copy.26
  176.4 2.1 reshape.88
  178.6 2.1 copy.27
  180.7 1.5 broadcast_in_dim.87
  182.2 2.3 select_reduce_fusion
  184.5 0.1 broadcast_in_dim_reshape.2
  184.6 10.3 %all-to-all-done = bf16[128,16,256]{2,1,0:T(8,128)(2,1)} async-done(((bf16[128,16,256]{2,1,0:T(8,128)(2,1)}), bf16[128,16,256]{2,1,0:T(8,128)(2,1)}, u32[]{:S(2)}, u32[]{:S(2)}) %all-to-all-start) | async-done | bytes 1048608 | tf_op jit(solution)/shard_map/all_to_all | solution.py:251
  194.9 1.8 fusion.24
  196.6 2.6 %fusion.34 = (bf16[256,256]{1,0:T(8,128)(2,1)}, f32[256,256]{1,0:T(8,128)}) fusion(f32[256,256]{1,0:T(8,128)S(1)} %fusion.24, bf16[2048,256]{1,0:T(8,128)(2,1)} %bitcast.8, f32[2048]{0:T(1024)S(1)} %broadcast_in_dim_reshape.2, s32[2048]{0:T(1024)S(1)} %broadcast_add_fusion, f32[2048]{0:T(1024)S(1)} %broadcast_subtract_fusion, s32[2048]{0:T(1024)S(1)} %select_n.62), kind=kOutput, calls=%fused_computation.55 | convolution fusion | flops 273285120 | bytes 1736704 | tf_op jit(solution)/shard_map/dot_general | solution.py:255
  199.2 0.0 all-gather.2.cloned.1.call-update
  199.2 40.5 %all-gather.2.cloned.1.call-done = bf16[4096,256]{1,0:T(8,128)(2,1)} async-done(((bf16[256,256]{1,0:T(8,128)(2,1)}), bf16[4096,256]{1,0:T(8,128)(2,1)}) %all-gather.2.cloned.1.call-update) | async-done | bytes 2097168 | tf_op jit(solution)/shard_map/all_gather | solution.py:256
  239.7 3.0 %copy.47 = bf16[4096,256]{1,0:T(8,128)(2,1)} copy(bf16[4096,256]{1,0:T(8,128)(2,1)} %all-gather.2.cloned.1.call-done) | data formatting | bytes 4194304
  (9 shorter events, 0.0 us)
Async XLA Ops:
  7.2 92.9 %all-reduce.2.cloned.1.call-start = ((), (), s32[]{:S(2)}) async-start(), calls=%async_computation.1 | async-start | bytes 2097152 | tf_op jit(solution)/shard_map/psum | solution.py:218
  34.6 10.5 %copy-start.1 = (s32[320,512]{1,0:T(8,128)S(1)}, s32[320,512]{1,0:T(8,128)}, u32[]{:S(2)}) copy-start(s32[320,512]{1,0:T(8,128)} %param.11) | copy-start | bytes 1966084
  47.6 3.2 %copy-start.2 = (s32[320,512]{1,0:T(8,128)S(1)}, s32[320,512]{1,0:T(8,128)}, u32[]{:S(2)}) copy-start(s32[320,512]{1,0:T(8,128)} %param.12) | copy-start | bytes 1966084
  55.3 3.8 %copy-start.4 = (s32[512,2]{0,1:T(2,128)S(1)}, s32[512,2]{0,1:T(2,128)}, u32[]{:S(2)}) copy-start(s32[512,2]{0,1:T(2,128)} %param.8) | copy-start | bytes 12292
  100.1 3.0 %copy-start = (f32[512,512]{1,0:T(8,128)S(1)}, f32[512,512]{1,0:T(8,128)}, u32[]{:S(2)}) copy-start(f32[512,512]{1,0:T(8,128)} %all-reduce.2.cloned.1.call-done) | copy-start | bytes 3145732
  169.8 6.4 %copy-start.3 = (f32[320,512]{1,0:T(8,128)S(1)}, f32[320,512]{1,0:T(8,128)}, u32[]{:S(2)}) copy-start(f32[320,512]{1,0:T(8,128)} %param.13) | copy-start | bytes 1966084
  169.8 25.1 %all-to-all-start = ((bf16[128,16,256]{2,1,0:T(8,128)(2,1)}), bf16[128,16,256]{2,1,0:T(8,128)(2,1)}, u32[]{:S(2)}, u32[]{:S(2)}) async-start(bf16[128,16,256]{2,1,0:T(8,128)(2,1)} %bitcast.7), calls=%async_computation | async-start | bytes 2097152 | tf_op jit(solution)/shard_map/all_to_all | solution.py:251
  176.0 63.7 %all-gather.2.cloned.1.call-start = ((), (), s32[]{:S(2)}) async-start(), calls=%async_computation.2 | async-start | bytes 2228224 | tf_op jit(solution)/shard_map/all_gather | solution.py:256
Sparse Core Ops, SparseCore 0:
  34.7 65.3 all-reduce.1
  199.3 40.3 all-gather.1

commit v3 on v2

--- a/solution.py
+++ b/solution.py
@@ -178,6 +178,166 @@
     )(images, posterior)
 
 
+def exchange_kernel(
+    pieces_ref, slot_ref, row_ref, part_ref, volume_ref, next_ref,
+    packed, got, insert, own_sem, out_sem, in_sem, send_a, recv_a, send_b, recv_b,
+):
+    torus = Torus()
+    slabs = lax.axis_size("slab")
+    devices = lax.axis_size("dom") * slabs
+    me = (torus.at["y"] * SIDE + torus.at["x"]) * slabs + torus.slab
+    width = pieces_ref.shape[1]
+    routes = range(len(ROUTES))
+
+    def device(number):
+        return (lax.div(number, slabs), lax.rem(number, slabs))
+
+    barrier = pltpu.get_barrier_semaphore()
+
+    @pl.loop(1, devices)
+    def _(k):
+        to = lax.rem(me + k, devices)
+        pl.semaphore_signal(barrier, inc=1, device_id=device(to), device_id_type=MESH)
+
+    block = RD
+    owners = block // CAP
+    numbers = lax.broadcasted_iota(jnp.int32, (block, pieces_ref.shape[0]), 0)
+    for b in range(devices // owners):
+        pick = (numbers + b * block == slot_ref[...]).astype(jnp.float32).astype(jnp.bfloat16)
+        value = jnp.dot(pick, pieces_ref[...], preferred_element_type=jnp.float32)
+        packed[b * owners : (b + 1) * owners] = value.astype(jnp.bfloat16).reshape(owners, CAP, width)
+    pl.semaphore_wait(barrier, devices - 1)
+
+    @pl.loop(1, devices)
+    def _(k):
+        to = lax.rem(me + k, devices)
+        pltpu.make_async_remote_copy(
+            src_ref=packed.at[to],
+            dst_ref=got.at[me],
+            send_sem=out_sem,
+            recv_sem=in_sem,
+            device_id=device(to),
+            device_id_type=MESH,
+        ).start()
+
+    own = pltpu.make_async_copy(packed.at[me], got.at[me], own_sem)
+    own.start()
+    lanes = row_ref.shape[1]
+    rows = lax.broadcasted_iota(jnp.int32, (RD, lanes), 0)
+    for b in range(row_ref.shape[0]):
+        row = row_ref[b : b + 1, :]
+        part = part_ref[b : b + 1, :]
+        weight = jnp.where(rows == row, 1.0 - part, 0.0) + jnp.where(rows == row + 1, part, 0.0)
+        high = weight.astype(jnp.bfloat16)
+        insert[0, :, b * lanes : (b + 1) * lanes] = high
+        insert[1, :, b * lanes : (b + 1) * lanes] = (weight - high.astype(jnp.float32)).astype(jnp.bfloat16)
+    own.wait()
+    others = got.at[pl.ds(0, devices - 1)]
+    pltpu.make_async_copy(others, others, in_sem).wait()
+    pieces = got[...].reshape(devices * CAP, width)
+    volume = jnp.dot(insert[0], pieces, preferred_element_type=jnp.float32)
+    volume = volume + jnp.dot(insert[1], pieces, preferred_element_type=jnp.float32)
+    volume_ref[...] = volume
+    part_rows = RD // len(ROUTES)
+    for q in routes:
+        next_ref[torus.at["y"], torus.at["x"], q] = volume[
+            q * part_rows : (q + 1) * part_rows
+        ].astype(jnp.bfloat16)
+
+    def origin(q, stage, hop):
+        axis, sign = ROUTES[q]
+        axis = axis if stage == 1 else other(axis)
+        return lax.rem(torus.at[axis] - sign * hop + 2 * SIDE, SIDE)
+
+    def place(q, first, second):
+        y, x = (second, first) if ROUTES[q][0] == "x" else (first, second)
+        return next_ref.at[y, x, q]
+
+    def hop_a(q, hop):
+        axis, sign = ROUTES[q]
+        spot = place(q, origin(q, 1, hop), torus.at[other(axis)])
+        return pltpu.make_async_remote_copy(
+            src_ref=spot,
+            dst_ref=spot,
+            send_sem=send_a.at[q, hop],
+            recv_sem=recv_a.at[q, hop],
+            device_id=torus.neighbour(axis, sign),
+            device_id_type=MESH,
+        )
+
+    def hop_b(q, hop, j):
+        axis, sign = ROUTES[q]
+        spot = place(q, origin(q, 1, j), origin(q, 2, hop))
+        return pltpu.make_async_remote_copy(
+            src_ref=spot,
+            dst_ref=spot,
+            send_sem=send_b.at[q, hop, j],
+            recv_sem=recv_b.at[q, hop, j],
+            device_id=torus.neighbour(other(axis), sign),
+            device_id_type=MESH,
+        )
+
+    for q in routes:
+        hop_a(q, 0).start()
+        hop_b(q, 0, 0).start()
+    for step in range(1, 2 * SIDE - 1):
+        for q in routes:
+            if step < SIDE:
+                hop_a(q, step - 1).wait_recv()
+                if step < SIDE - 1:
+                    hop_a(q, step).start()
+                hop_b(q, 0, step).start()
+        for q in routes:
+            for hop in range(SIDE - 1):
+                j = step - 1 - hop
+                if 0 <= j < SIDE:
+                    hop_b(q, hop, j).wait_recv()
+                    if hop < SIDE - 2:
+                        hop_b(q, hop + 1, j).start()
+    for q in routes:
+        for hop in range(SIDE - 1):
+            hop_a(q, hop).wait_send()
+            for j in range(SIDE):
+                hop_b(q, hop, j).wait_send()
+    sent = packed.at[pl.ds(0, devices - 1)]
+    pltpu.make_async_copy(sent, sent, out_sem).wait()
+
+
+def exchanged(pieces, slot, row, part, devices):
+    width = pieces.shape[1]
+    routes = len(ROUTES)
+    hops = SIDE - 1
+    part_rows = RD // routes
+    vmem = pl.BlockSpec(memory_space=pltpu.VMEM)
+    sems_a = pltpu.SemaphoreType.DMA((routes, hops))
+    sems_b = pltpu.SemaphoreType.DMA((routes, hops, SIDE))
+    return pl.pallas_call(
+        exchange_kernel,
+        out_shape=(
+            jax.ShapeDtypeStruct((RD, width), jnp.float32),
+            jax.ShapeDtypeStruct((SIDE, SIDE, routes, part_rows, width), jnp.bfloat16),
+        ),
+        in_specs=[vmem] * 4,
+        out_specs=(vmem, vmem),
+        scratch_shapes=[
+            pltpu.VMEM((devices, CAP, width), jnp.bfloat16),
+            pltpu.VMEM((devices, CAP, width), jnp.bfloat16),
+            pltpu.VMEM((2, RD, devices * CAP), jnp.bfloat16),
+            pltpu.SemaphoreType.DMA,
+            pltpu.SemaphoreType.DMA,
+            pltpu.SemaphoreType.DMA,
+            sems_a,
+            sems_a,
+            sems_b,
+            sems_b,
+        ],
+        compiler_params=pltpu.CompilerParams(
+            collective_id=1, has_side_effects=True, vmem_limit_bytes=32 * 1024 * 1024
+        ),
+        name="exchange_pieces",
+    )(pieces, slot, row, part)
+
+
 def send_slots(dests, devices):
     count = dests.shape[0]
     onehot = dests[:, None] == jnp.arange(devices, dtype=jnp.int32)[None, :]
@@ -229,11 +389,6 @@
         destination, (slab_pos * groups, dom_pos * share), (groups, share)
     )
     slot = send_slots(my_dest.reshape(-1), devices)
-    pack = jnp.arange(devices * CAP, dtype=jnp.int32)[:, None] == slot[None, :]
-    packed = jnp.dot(
-        pack.astype(jnp.bfloat16), pieces, preferred_element_type=jnp.float32
-    ).astype(jnp.bfloat16)
-
     def by_source(table):
         table = table.reshape(slab_size, groups, dom_size, share).transpose(2, 0, 1, 3)
         return table.reshape(devices, share * groups)
@@ -242,18 +397,14 @@
         (by_source(row_index), by_source(fraction)), by_source(destination), me
     )
     row = jnp.where(filled, row, -2)
-    rows = jnp.arange(RD, dtype=jnp.int32)[:, None]
-    insert = jnp.where(row[None, :] == rows, 1.0 - part[None, :], 0.0)
-    insert = insert + jnp.where(row[None, :] + 1 == rows, part[None, :], 0.0)
-    insert_high = insert.astype(jnp.bfloat16)
-    insert_low = (insert - insert_high.astype(jnp.float32)).astype(jnp.bfloat16)
-
-    got = lax.all_to_all(
-        packed.reshape(devices, CAP, row_width), ("dom", "slab"), 0, 0, tiled=True
-    ).reshape(devices * CAP, row_width)
-    volume = jnp.dot(insert_high, got, preferred_element_type=jnp.float32)
-    volume = volume + jnp.dot(insert_low, got, preferred_element_type=jnp.float32)
-    next_slab = lax.all_gather(volume.astype(jnp.bfloat16), "dom", axis=0, tiled=True)
+    volume, next_slab = exchanged(
+        pieces,
+        slot[None, :],
+        row.reshape(dom_size, -1),
+        part.reshape(dom_size, -1),
+        devices,
+    )
+    next_slab = next_slab.reshape(dom_size * RD, row_width)
     return (volume, next_slab)
 
 

time: 250 us -> 224 us (0.90)
  waiting for transfers between devices: 88.2 us -> 27.5 us
  Pallas kernels: 63.4 us -> 110 us
  matrix products: 25.7 us -> 18.3 us
  starting transfers between devices: 6.3 us -> 0.04 us
    pallas_call x0 -> x1, Pallas kernels: none -> 46.8 us  [exchanged(): pl.pallas_call(exchange_kernel, out_shape=(jax.ShapeDtypeStruct((RD, widt...]
    all_gather x1 -> x0, waiting for transfers between devices: 40.5 us -> none  [shards(): lax.all_gather(volume.astype(jnp.bfloat16), 'dom', axis=0, tiled=True)]
    all_to_all x1 -> x0, waiting for transfers between devices: 10.3 us -> none  [shards(): lax.all_to_all(packed.reshape(devices, CAP, row_width), ('dom', 'slab'),...]
    psum x1, waiting for transfers between devices: 37.4 us -> 27.5 us  [shards(): scores = lax.psum(partial_value, 'slab')]
    dot_general x3 -> x0, matrix products: 7.33 us -> none  [the longest x1 3 us: shards(): jnp.dot(pack.astype(jnp.bfloat16), pieces, preferred_element_type=jnp.flo...]
    all_to_all x1 -> x0, starting transfers between devices: 6.22 us -> none  [shards(): lax.all_to_all(packed.reshape(devices, CAP, row_width), ('dom', 'slab'),...]
    unnamed x14 -> x11, local copies, waits for them, and re-layouts: 14.1 us -> 14.2 us
  transfers between devices with their start and end apart: 3 -> 1, of which waited for: 3 -> 1; matrix products, arithmetic and copies ran while one was open for 15% -> 17% of each run, Pallas kernels for 0% -> 0%
where the time goes in v3:
time: 224 us; the launch traced here: 223 us
  Pallas kernels  110 us (49%)
  local copies, waits for them, and re-layouts  30 us (13%)
  waiting for transfers between devices  27.5 us (12%)
  other arithmetic  23.5 us (10%)
  matrix products  18.3 us (8%)
  between operations  14.2 us (6%)
    pallas_call x1, Pallas kernels, summed_slices(): pl.pallas_call(sum_kernel, out_shape=jax.ShapeDtypeStruct((groups, share,...  63.1 us
    pallas_call x1, Pallas kernels, exchanged(): pl.pallas_call(exchange_kernel, out_shape=(jax.ShapeDtypeStruct((RD, widt...  46.8 us
    psum x1, waiting for transfers between devices, shards(): scores = lax.psum(partial_value, 'slab')  27.5 us
    dot_general x1, matrix products, shards(): lax.dot_general(weighted, particles, (((1, 2), (1, 2)), ((), ())), prefer...  16.8 us
    unnamed x11, local copies, waits for them, and re-layouts  14.2 us
    convert_element_type x1, other arithmetic, shards(): (references.astype(jnp.float32) * inv_noise[None, :, None]).astype(jnp.bf...  10.6 us
    reduce_sum x2, other arithmetic, received_slots(): jnp.sum(jnp.where(chosen, t[:, None, :], 0), axis=2).reshape(-1)  5.69 us
    transpose x2, local copies, waits for them, and re-layouts, by_source(): table.reshape(slab_size, groups, dom_size, share).transpose(2, 0, 1, 3)  4.48 us
  transfers between devices with their start and end apart: 1, of which 1 were waited for; matrix products, arithmetic and copies ran while one was open for 17% of the time, Pallas kernels for 0%

profile of v3, /device:TPU:0, one launch (start us, length us, event | category | flops | bytes accessed | tf_op | source)
XLA Modules:
  0.0 223.5 jit_solution(10558114788787012990)
XLA Ops:
  7.2 0.0 all-reduce.2.cloned.1.call-start
  7.2 10.6 %multiply_convert_fusion = bf16[512,40,256]{2,1,0:T(8,128)(2,1)} fusion(bf16[512,40,256]{2,1,0:T(8,128)(2,1)} %param.9, f32[40]{0:T(128)} %param.10), kind=kLoop, calls=%fused_computation | loop fusion | flops 15728640 | bytes 20971680 | tf_op jit(solution)/shard_map/convert_element_type | solution.py:374
  17.8 16.8 %fusion.9 = f32[512,512]{1,0:T(8,128)} fusion(bf16[512,40,256]{2,1,0:T(8,128)(2,1)} %param.7, bf16[512,40,256]{2,1,0:T(8,128)(2,1)} %multiply_convert_fusion), kind=kOutput, calls=%fused_computation.17 | convolution fusion | flops 5368709120 | bytes 22020096 | tf_op jit(solution)/shard_map/dot_general | solution.py:375
  34.6 0.0 all-reduce.2.cloned.1.call-update
  34.6 0.0 copy-start
  34.6 10.5 %copy.40 = bf16[512,40,256]{2,0,1:T(8,128)(2,1)} copy(bf16[512,40,256]{2,1,0:T(8,128)(2,1)} %param.7) | data formatting | bytes 20971520 | tf_op args[0]
  45.1 0.0 copy-start.1
  45.1 0.0 copy-done
  45.1 0.1 broadcast_multiply_fusion
  45.2 0.1 eq.59
  45.3 0.9 fusion.14
  46.2 0.1 mul.39
  46.3 0.1 broadcast_compare_fusion
  46.4 0.3 copy.25
  46.8 0.9 eq.65
  47.7 1.4 copy.26
  49.1 1.1 eq.67
  50.2 0.6 fusion.8
  50.8 0.0 copy-done.1
  50.8 0.3 copy.27
  51.1 2.1 reshape.75
  53.2 2.1 copy.28
  55.3 0.0 copy-start.2
  55.3 1.5 broadcast_in_dim.64
  56.9 2.3 %fusion.2 = pred[128,16]{1,0:T(8,128)(4,1)S(1)} fusion(s32[128,1280]{1,0:T(8,128)S(1)} %fusion.8), kind=kLoop, calls=%fused_computation.6 | loop fusion | flops 5240832 | bytes 657408 | tf_op jit(solution)/shard_map/reduce_or | solution.py:360
  59.1 3.4 %select_reduce_fusion.1 = s32[128,16]{1,0:T(8,128)S(1)} fusion(s32[128,1280]{1,0:T(8,128)} %broadcast_in_dim.64, s32[128,1280]{1,0:T(8,128)S(1)} %fusion.8), kind=kLoop, calls=%fused_computation.4 | loop fusion | flops 7862272 | bytes 1318912 | tf_op jit(solution)/shard_map/reduce_sum | solution.py:359
  62.5 0.1 select_n.55.row_ref
  62.6 1.4 copy.29
  64.0 2.1 reshape.76
  66.1 2.4 %copy.30 = f32[16,8,40,32]{3,2,1,0:T(8,128)S(1)} copy(f32[16,8,40,32]{2,1,3,0:T(8,128)} %bitcast.28) | data formatting | bytes 1310720 | tf_op jit(solution)/shard_map/transpose | solution.py:393
  68.5 1.5 broadcast_in_dim.68
  70.0 2.3 %select_reduce_fusion = f32[128,16]{1,0:T(8,128)S(1)} fusion(f32[128,1280]{1,0:T(8,128)} %broadcast_in_dim.68, s32[128,1280]{1,0:T(8,128)S(1)} %fusion.8), kind=kLoop, calls=%fused_computation.3 | loop fusion | flops 7862272 | bytes 1318912 | tf_op jit(solution)/shard_map/reduce_sum | solution.py:359
  72.3 0.1 reshape_reshape.3.part_ref
  72.4 0.0 copy-done.2
  72.4 0.2 compare_reduce_fusion
  72.7 27.5 %all-reduce.2.cloned.1.call-done = f32[512,512]{1,0:T(8,128)} async-done(((f32[512,512]{1,0:T(8,128)}), f32[512,512]{1,0:T(8,128)}) %all-reduce.2.cloned.1.call-update) | async-done | bytes 1048592 | tf_op jit(solution)/shard_map/psum | solution.py:378
  100.2 1.4 fusion.16
  101.6 1.5 fusion.15
  103.1 1.5 divide_convert_fusion.post_ref
  104.7 63.1 %sum_slices.1 = bf16[40,32,256]{2,1,0:T(8,128)(2,1)S(1)} custom-call(bf16[40,512,256]{2,1,0:T(8,128)(2,1)} %bitcast.26, bf16[512,512]{1,0:T(8,128)(2,1)S(1)} %divide_convert_fusion.post_ref), custom_call_target="tpu_custom_call" | custom-call | tf_op jit(solution)/shard_map/sum_slices/pallas_call | solution.py:155
  167.8 46.8 %exchange_pieces.1 = (f32[256,256]{1,0:T(8,128)S(1)}, bf16[4,4,4,64,256]{4,3,2,1,0:T(8,128)(2,1)S(1)}) custom-call(bf16[1280,256]{1,0:T(8,128)(2,1)S(1)} %bitcast.24, s32[1,1280]{1,0:T(1,128)S(1)} %reshape_add_fusion.slot_ref, s32[16,128]{1,0:T(8,128)S(1)} %select_n.55.row_ref, f32[16,128]{1,0:T(8,128)S(1)} %reshape_reshape.3.part_ref), custom_call_target="tpu_custom_call" | custom-call | tf_op jit(solution)/shard_map/exchange_pieces/pallas_call | solution.py:314
  214.6 0.7 copy.46
  215.3 1.3 copy.47
  (4 shorter events, 0.0 us)
Async XLA Ops:
  7.2 93.0 %all-reduce.2.cloned.1.call-start = ((), (), s32[]{:S(2)}) async-start(), calls=%async_computation | async-start | bytes 2097152 | tf_op jit(solution)/shard_map/psum | solution.py:378
  34.6 10.5 %copy-start = (s32[320,512]{1,0:T(8,128)S(1)}, s32[320,512]{1,0:T(8,128)}, u32[]{:S(2)}) copy-start(s32[320,512]{1,0:T(8,128)} %param.11) | copy-start | bytes 1966084
  45.1 5.7 %copy-start.1 = (s32[320,512]{1,0:T(8,128)S(1)}, s32[320,512]{1,0:T(8,128)}, u32[]{:S(2)}) copy-start(s32[320,512]{1,0:T(8,128)} %param.12) | copy-start | bytes 1966084
  55.3 17.1 %copy-start.2 = (s32[512,2]{0,1:T(2,128)S(1)}, s32[512,2]{0,1:T(2,128)}, u32[]{:S(2)}) copy-start(s32[512,2]{0,1:T(2,128)} %param.8) | copy-start | bytes 12292
Sparse Core Ops, SparseCore 0:
  34.7 65.3 all-reduce.1

commit v4 on v3

--- a/solution.py
+++ b/solution.py
@@ -178,6 +178,197 @@
     )(images, posterior)
 
 
+def slot_tables(dest_ref, row_ref, part_ref, me, counts, rows_at, parts_at, row_out, part_out):
+    slabs = lax.axis_size("slab")
+    orients = dest_ref.shape[1]
+    groups = dest_ref.shape[0] // slabs
+    doms = row_out.shape[0]
+    shift = (orients // doms).bit_length() - 1
+    here = lax.broadcasted_iota(jnp.int32, (orients, orients), 0)
+    there = lax.broadcasted_iota(jnp.int32, (orients, orients), 1)
+    same = lax.shift_right_logical(here, shift) == lax.shift_right_logical(there, shift)
+    share = same.astype(jnp.float32).astype(jnp.bfloat16)
+    before = jnp.where(same & (here < there), 1.0, 0.0).astype(jnp.bfloat16)
+    mask = (dest_ref[...] == me).astype(jnp.float32).astype(jnp.bfloat16)
+    counts[0] = jnp.dot(mask, before, preferred_element_type=jnp.float32)
+    counts[1] = jnp.dot(mask, share, preferred_element_type=jnp.float32)
+    lower = lax.broadcasted_iota(jnp.int32, (groups, groups), 0) > lax.broadcasted_iota(
+        jnp.int32, (groups, groups), 1
+    )
+    lower = lower.astype(jnp.float32).astype(jnp.bfloat16)
+
+    @pl.loop(0, slabs)
+    def _(s):
+        span = pl.ds(pl.multiple_of(s * groups, groups), groups)
+        above = jnp.dot(
+            lower, counts[1, span].astype(jnp.bfloat16), preferred_element_type=jnp.float32
+        )
+        rank = jnp.where(dest_ref[span] == me, counts[0, span] + above, -1.0)
+        row = row_ref[span].astype(jnp.float32) + 1.0
+        part = part_ref[span]
+        found_rows = []
+        found_parts = []
+        for j in range(CAP):
+            chosen = rank == j
+            found_rows.append(jnp.sum(jnp.where(chosen, row, 0.0), axis=0, keepdims=True))
+            found_parts.append(jnp.sum(jnp.where(chosen, part, 0.0), axis=0, keepdims=True))
+        slots = pl.ds(pl.multiple_of(s * CAP, CAP), CAP)
+        rows_at[slots] = jnp.concatenate(found_rows, axis=0)
+        parts_at[slots] = jnp.concatenate(found_parts, axis=0)
+
+    owner = lax.shift_right_logical(lax.broadcasted_iota(jnp.int32, (doms, orients), 1), shift)
+    gather = (owner == lax.broadcasted_iota(jnp.int32, (doms, orients), 0)).astype(jnp.float32)
+    over_lanes = (((1,), (1,)), ((), ()))
+    for found, out in ((rows_at, row_out), (parts_at, part_out)):
+        out[...] = lax.dot_general(
+            gather, found[...], over_lanes,
+            precision=lax.Precision.HIGHEST, preferred_element_type=jnp.float32,
+        )
+    row_out[...] = row_out[...] - 1.0
+
+
+def posterior_kernel(
+    scores_ref, blocks_ref, dest_ref, row_ref, part_ref, post_ref, row_out, part_out,
+    mine, from_mate, total, from_chips, found, counts, rows_at, parts_at,
+    mate_send, mate_recv, chip_send, chip_recv, back_send, back_recv, last_send, last_recv,
+):
+    dom = lax.axis_index("dom")
+    slab = lax.axis_index("slab")
+    slabs = lax.axis_size("slab")
+    chips = slabs // 2
+    chip = lax.div(slab, 2)
+    core = lax.rem(slab, 2)
+    mate = (dom, 2 * chip + 1 - core)
+    me = dom * slabs + slab
+    count = mine.shape[2]
+
+    def peer(step):
+        return (dom, 2 * lax.rem(chip + step, chips) + core)
+
+    barrier = pltpu.get_barrier_semaphore()
+    pl.semaphore_signal(barrier, inc=1, device_id=mate, device_id_type=MESH)
+    for step in range(1, chips):
+        pl.semaphore_signal(barrier, inc=1, device_id=peer(step), device_id_type=MESH)
+
+    def picked(span, which):
+        chosen = blocks_ref[span, which : which + 1]
+        value = scores_ref[span, 0:OB]
+        for b in range(1, scores_ref.shape[1] // OB):
+            value = jnp.where(chosen == b, scores_ref[span, b * OB : (b + 1) * OB], value)
+        return value
+
+    for s in range(slabs):
+        span = pl.ds(s * count, count)
+        for which in range(2):
+            mine[s % 2, s // 2, :, which * OB : (which + 1) * OB] = picked(span, which)
+    pl.semaphore_wait(barrier, chips)
+    to_mate = pltpu.make_async_remote_copy(
+        src_ref=mine.at[1 - core],
+        dst_ref=from_mate,
+        send_sem=mate_send,
+        recv_sem=mate_recv,
+        device_id=mate,
+        device_id_type=MESH,
+    )
+    to_mate.start()
+    to_mate.wait_recv()
+    total[...] = mine[core] + from_mate[...]
+
+    def to_chip(step):
+        return pltpu.make_async_remote_copy(
+            src_ref=total.at[lax.rem(chip + step, chips)],
+            dst_ref=from_chips.at[step - 1],
+            send_sem=chip_send.at[step - 1],
+            recv_sem=chip_recv.at[step - 1],
+            device_id=peer(step),
+            device_id_type=MESH,
+        )
+
+    for step in range(1, chips):
+        to_chip(step).start()
+    slot_tables(dest_ref, row_ref, part_ref, me, counts, rows_at, parts_at, row_out, part_out)
+    for step in range(1, chips):
+        to_chip(step).wait_recv()
+    scores = total[chip]
+    for step in range(1, chips):
+        scores = scores + from_chips[step - 1]
+    weights = jnp.exp(scores - jnp.max(scores, axis=1, keepdims=True))
+    found[chip, core] = (weights / jnp.sum(weights, axis=1, keepdims=True)).astype(jnp.bfloat16)
+
+    def back(step):
+        return pltpu.make_async_remote_copy(
+            src_ref=found.at[chip, core],
+            dst_ref=found.at[chip, core],
+            send_sem=back_send.at[step - 1],
+            recv_sem=back_recv.at[step - 1],
+            device_id=peer(step),
+            device_id_type=MESH,
+        )
+
+    for step in range(1, chips):
+        back(step).start()
+    for step in range(1, chips):
+        back(step).wait_recv()
+    last = pltpu.make_async_remote_copy(
+        src_ref=found.at[:, core],
+        dst_ref=found.at[:, core],
+        send_sem=last_send,
+        recv_sem=last_recv,
+        device_id=mate,
+        device_id_type=MESH,
+    )
+    last.start()
+    last.wait_recv()
+    everyone = found[...].astype(jnp.float32).reshape(slabs * count, 2 * OB)
+    first, second = blocks_ref[:, 0:1], blocks_ref[:, 1:2]
+    for b in range(scores_ref.shape[1] // OB):
+        value = jnp.where(first == b, everyone[:, :OB], 0.0)
+        value = jnp.where(second == b, everyone[:, OB:], value)
+        post_ref[b * OB : (b + 1) * OB, :] = value.T.astype(jnp.bfloat16)
+    to_mate.wait_send()
+    last.wait_send()
+    for step in range(1, chips):
+        to_chip(step).wait_send()
+        back(step).wait_send()
+
+
+def posteriors(scores, blocks, destination, row_index, fraction, doms, slabs):
+    particles, orients = scores.shape
+    chips = slabs // 2
+    count = particles // slabs
+    vmem = pl.BlockSpec(memory_space=pltpu.VMEM)
+    table = jax.ShapeDtypeStruct((doms, slabs * CAP), jnp.float32)
+    dma = pltpu.SemaphoreType.DMA
+    return pl.pallas_call(
+        posterior_kernel,
+        out_shape=(jax.ShapeDtypeStruct((orients, particles), jnp.bfloat16), table, table),
+        in_specs=[vmem] * 5,
+        out_specs=(vmem,) * 3,
+        scratch_shapes=[
+            pltpu.VMEM((2, chips, count, 2 * OB), jnp.float32),
+            pltpu.VMEM((chips, count, 2 * OB), jnp.float32),
+            pltpu.VMEM((chips, count, 2 * OB), jnp.float32),
+            pltpu.VMEM((chips - 1, count, 2 * OB), jnp.float32),
+            pltpu.VMEM((chips, 2, count, 2 * OB), jnp.bfloat16),
+            pltpu.VMEM((2,) + destination.shape, jnp.float32),
+            pltpu.VMEM((slabs * CAP, orients), jnp.float32),
+            pltpu.VMEM((slabs * CAP, orients), jnp.float32),
+            dma,
+            dma,
+            dma((chips - 1,)),
+            dma((chips - 1,)),
+            dma((chips - 1,)),
+            dma((chips - 1,)),
+            dma,
+            dma,
+        ],
+        compiler_params=pltpu.CompilerParams(
+            collective_id=2, has_side_effects=True, vmem_limit_bytes=32 * 1024 * 1024
+        ),
+        name="posteriors",
+    )(scores, blocks, destination, row_index, fraction)
+
+
 def exchange_kernel(
     pieces_ref, slot_ref, row_ref, part_ref, volume_ref, next_ref,
     packed, got, insert, own_sem, out_sem, in_sem, send_a, recv_a, send_b, recv_b,
@@ -223,7 +414,7 @@
     own = pltpu.make_async_copy(packed.at[me], got.at[me], own_sem)
     own.start()
     lanes = row_ref.shape[1]
-    rows = lax.broadcasted_iota(jnp.int32, (RD, lanes), 0)
+    rows = lax.broadcasted_iota(jnp.int32, (RD, lanes), 0).astype(jnp.float32)
     for b in range(row_ref.shape[0]):
         row = row_ref[b : b + 1, :]
         part = part_ref[b : b + 1, :]
@@ -348,19 +539,6 @@
     return dests * CAP + rank
 
 
-def received_slots(tables, dests, me):
-    count = dests.shape[1]
-    mask = dests == me
-    place = jnp.arange(count, dtype=jnp.int32)
-    before = (place[:, None] < place[None, :]).astype(jnp.bfloat16)
-    rank = jnp.dot(mask.astype(jnp.bfloat16), before, preferred_element_type=jnp.float32)
-    rank = jnp.where(mask, rank.astype(jnp.int32), -1)
-    chosen = rank[:, None, :] == jnp.arange(CAP, dtype=jnp.int32)[None, :, None]
-    found = [jnp.sum(jnp.where(chosen, t[:, None, :], 0), axis=2).reshape(-1) for t in tables]
-    filled = jnp.any(chosen, axis=2).reshape(-1)
-    return found, filled
-
-
 def shards(particles, blocks, references, inv_noise, destination, row_index, fraction):
     particle_count, groups, row_width = particles.shape
     orients = references.shape[0]
@@ -369,19 +547,14 @@
     devices = dom_size * slab_size
     dom_pos = lax.axis_index("dom")
     slab_pos = lax.axis_index("slab")
-    me = dom_pos * slab_size + slab_pos
     share = orients // dom_size
     weighted = (references.astype(jnp.float32) * inv_noise[None, :, None]).astype(jnp.bfloat16)
-    partial_value = lax.dot_general(
-        weighted, particles, (((1, 2), (1, 2)), ((), ())), preferred_element_type=jnp.float32
-    )
-    scores = lax.psum(partial_value, "slab")
-    block_of = jnp.arange(orients, dtype=jnp.int32) // OB
-    allowed = jnp.any(blocks.T[:, None, :] == block_of[None, :, None], axis=0)
-    masked = jnp.where(allowed, scores, -jnp.inf)
-    highest = jnp.max(masked, axis=0, keepdims=True)
-    weights = jnp.where(allowed, jnp.exp(masked - highest), 0.0)
-    posterior = (weights / jnp.sum(weights, axis=0, keepdims=True)).astype(jnp.bfloat16)
+    scores = lax.dot_general(
+        particles, weighted, (((1, 2), (1, 2)), ((), ())), preferred_element_type=jnp.float32
+    )
+    posterior, row, part = posteriors(
+        scores, blocks, destination, row_index, fraction, dom_size, slab_size
+    )
     pieces = summed_slices(particles.transpose(1, 0, 2), posterior, share)
     pieces = pieces.reshape(groups * share, row_width)
 
@@ -389,21 +562,7 @@
         destination, (slab_pos * groups, dom_pos * share), (groups, share)
     )
     slot = send_slots(my_dest.reshape(-1), devices)
-    def by_source(table):
-        table = table.reshape(slab_size, groups, dom_size, share).transpose(2, 0, 1, 3)
-        return table.reshape(devices, share * groups)
-
-    (row, part), filled = received_slots(
-        (by_source(row_index), by_source(fraction)), by_source(destination), me
-    )
-    row = jnp.where(filled, row, -2)
-    volume, next_slab = exchanged(
-        pieces,
-        slot[None, :],
-        row.reshape(dom_size, -1),
-        part.reshape(dom_size, -1),
-        devices,
-    )
+    volume, next_slab = exchanged(pieces, slot[None, :], row, part, devices)
     next_slab = next_slab.reshape(dom_size * RD, row_width)
     return (volume, next_slab)
 

time: 224 us -> 170 us (0.76)
  waiting for transfers between devices: 27.5 us -> 0 us
  Pallas kernels: 110 us -> 127 us
  local copies, waits for them, and re-layouts: 30 us -> 13.6 us
  between operations: 14.2 us -> 0.74 us
  other arithmetic: 23.5 us -> 11.4 us
    psum x1 -> x0, waiting for transfers between devices: 27.5 us -> none  [shards(): scores = lax.psum(partial_value, 'slab')]
    pallas_call x0 -> x1, Pallas kernels: none -> 16.2 us  [posteriors(): pl.pallas_call(posterior_kernel, out_shape=(jax.ShapeDtypeStruct((orients...]
    reduce_sum x3 -> x0, other arithmetic: 7.22 us -> none  [the longest x2 5.69 us: received_slots(): jnp.sum(jnp.where(chosen, t[:, None, :], 0), axis=2).reshape(-1)]
    transpose x2 -> x0, local copies, waits for them, and re-layouts: 4.48 us -> none  [by_source(): table.reshape(slab_size, groups, dom_size, share).transpose(2, 0, 1, 3)]
    reshape x2 -> x0, local copies, waits for them, and re-layouts: 4.25 us -> none  [by_source(): table.reshape(slab_size, groups, dom_size, share).transpose(2, 0, 1, 3)]
    eq x4 -> x0, local copies, waits for them, and re-layouts: 3.78 us -> none  [received_slots(): mask = dests == me]
    broadcast_in_dim x2 -> x0, local copies, waits for them, and re-layouts: 3.01 us -> none  [received_slots(): jnp.where(chosen, t[:, None, :], 0)]
    reduce_or x2 -> x0, other arithmetic: 2.52 us -> none  [the longest x1 2.28 us: received_slots(): filled = jnp.any(chosen, axis=2).reshape(-1)]
  transfers between devices with their start and end apart: 1 -> 0, of which waited for: 1 -> 0; matrix products, arithmetic and copies ran while one was open for 17% -> 0% of each run, Pallas kernels for 0% -> 0%
where the time goes in v4:
time: 170 us
  Pallas kernels  127 us (75%)
  matrix products  17.3 us (10%)
  local copies, waits for them, and re-layouts  13.6 us (8%)
  other arithmetic  11.4 us (7%)
    pallas_call x1, Pallas kernels, summed_slices(): pl.pallas_call(sum_kernel, out_shape=jax.ShapeDtypeStruct((groups, share,...  63.9 us
    pallas_call x1, Pallas kernels, exchanged(): pl.pallas_call(exchange_kernel, out_shape=(jax.ShapeDtypeStruct((RD, widt...  46.8 us
    dot_general x1, matrix products, shards(): lax.dot_general(particles, weighted, (((1, 2), (1, 2)), ((), ())), prefer...  16.4 us
    pallas_call x1, Pallas kernels, posteriors(): pl.pallas_call(posterior_kernel, out_shape=(jax.ShapeDtypeStruct((orients...  16.2 us
    unnamed x16, local copies, waits for them, and re-layouts  13.4 us
    convert_element_type x1, other arithmetic, shards(): (references.astype(jnp.float32) * inv_noise[None, :, None]).astype(jnp.bf...  10.5 us

profile of v4, /device:TPU:0, one launch (start us, length us, event | category | flops | bytes accessed | tf_op | source)
XLA Modules:
  0.0 169.9 jit_solution(14248247340645860794)
XLA Ops:
  0.6 0.8 broadcast_multiply_fusion
  1.4 0.1 eq.15
  1.5 0.9 fusion.10
  2.5 0.1 mul.36
  2.6 10.5 %multiply_convert_fusion = bf16[512,40,256]{2,1,0:T(8,128)(2,1)} fusion(bf16[512,40,256]{2,1,0:T(8,128)(2,1)} %param.9, f32[40]{0:T(128)} %param.10), kind=kLoop, calls=%fused_computation | loop fusion | flops 15728640 | bytes 20971680 | tf_op jit(solution)/shard_map/convert_element_type | solution.py:551
  13.1 0.0 copy-start.5
  13.1 0.0 copy-start
  13.1 0.0 copy-start.1
  13.1 0.0 copy-start.2
  13.1 16.4 %fusion.5.scores_ref = f32[512,512]{1,0:T(8,128)S(1)} fusion(bf16[512,40,256]{2,1,0:T(8,128)(2,1)} %param.7, bf16[512,40,256]{2,1,0:T(8,128)(2,1)} %multiply_convert_fusion), kind=kOutput, calls=%fused_computation.8 | convolution fusion | flops 5368709120 | bytes 22020096 | tf_op jit(solution)/shard_map/dot_general | solution.py:552
  29.5 0.0 copy-done.5
  29.5 0.1 copy.18.blocks_ref
  29.7 0.0 copy-done
  29.7 0.0 copy-done.1
  29.7 0.0 copy-done.2
  29.7 16.2 %posteriors.1 = (bf16[512,512]{1,0:T(8,128)(2,1)S(1)}, f32[16,128]{1,0:T(8,128)S(1)}, f32[16,128]{1,0:T(8,128)S(1)}) custom-call(f32[512,512]{1,0:T(8,128)S(1)} %fusion.5.scores_ref, s32[512,2]{1,0:T(8,128)S(1)} %copy.18.blocks_ref, s32[320,512]{1,0:T(8,128)S(1)} %copy-done, s32[320,512]{1,0:T(8,128)S(1)} %copy-done.1, f32[320,512]{1,0:T(8,128)S(1)} %copy-done.2), custom_call_target="tpu_custom_call" | custom-call | tf_op jit(solution)/shard_map/posteriors/pallas_call | solution.py:342
  45.9 0.0 copy-start.3
  45.9 0.8 copy-done.3
  46.7 0.0 copy-start.4
  46.7 10.5 %copy.30 = bf16[512,40,256]{2,0,1:T(8,128)(2,1)} copy(bf16[512,40,256]{2,1,0:T(8,128)(2,1)} %param.7) | data formatting | bytes 20971520 | tf_op args[0]
  57.1 0.0 copy-done.4
  57.1 63.9 %sum_slices.1 = bf16[40,32,256]{2,1,0:T(8,128)(2,1)S(1)} custom-call(bf16[40,512,256]{2,1,0:T(8,128)(2,1)} %bitcast.11, bf16[512,512]{1,0:T(8,128)(2,1)S(1)} %copy-done.4), custom_call_target="tpu_custom_call" | custom-call | tf_op jit(solution)/shard_map/sum_slices/pallas_call | solution.py:155
  121.0 46.8 %exchange_pieces.1 = (f32[256,256]{1,0:T(8,128)S(1)}, bf16[4,4,4,64,256]{4,3,2,1,0:T(8,128)(2,1)S(1)}) custom-call(bf16[1280,256]{1,0:T(8,128)(2,1)S(1)} %bitcast.9, s32[1,1280]{1,0:T(1,128)S(1)} %reshape_add_fusion.slot_ref, f32[16,128]{1,0:T(8,128)S(1)} %get-tuple-element.8.row_ref, f32[16,128]{1,0:T(8,128)S(1)} %get-tuple-element.9.part_ref), custom_call_target="tpu_custom_call" | custom-call | tf_op jit(solution)/shard_map/exchange_pieces/pallas_call | solution.py:505
  167.8 0.7 copy.33
  168.5 1.3 copy.34
  (2 shorter events, 0.0 us)
Async XLA Ops:
  13.1 16.4 %copy-start.5 = (s32[512,2]{0,1:T(2,128)S(1)}, s32[512,2]{0,1:T(2,128)}, u32[]{:S(2)}) copy-start(s32[512,2]{0,1:T(2,128)} %param.8) | copy-start | bytes 12292
  13.1 16.6 %copy-start = (s32[320,512]{1,0:T(8,128)S(1)}, s32[320,512]{1,0:T(8,128)}, u32[]{:S(2)}) copy-start(s32[320,512]{1,0:T(8,128)} %dest_ref.1) | copy-start | bytes 1966084
  13.1 16.6 %copy-start.1 = (s32[320,512]{1,0:T(8,128)S(1)}, s32[320,512]{1,0:T(8,128)}, u32[]{:S(2)}) copy-start(s32[320,512]{1,0:T(8,128)} %row_ref.1) | copy-start | bytes 1966084
  13.1 16.6 %copy-start.2 = (f32[320,512]{1,0:T(8,128)S(1)}, f32[320,512]{1,0:T(8,128)}, u32[]{:S(2)}) copy-start(f32[320,512]{1,0:T(8,128)} %part_ref.1) | copy-start | bytes 1966084
  45.9 0.8 copy-start.3
  46.7 10.5 %copy-start.4 = (bf16[512,512]{1,0:T(8,128)(2,1)S(1)}, bf16[512,512]{1,0:T(8,128)(2,1)}, u32[]{:S(2)}) copy-start(bf16[512,512]{1,0:T(8,128)(2,1)} %copy-done.3) | copy-start | bytes 1572868

commit v5 on v3

--- a/solution.py
+++ b/solution.py
@@ -13,6 +13,9 @@
 CAP = 16
 SIDE = 4
 CHUNKS = 5
+TILE = 8
+ROWS = 16
+BAND = 256
 ROUTES = (("x", 1), ("x", -1), ("y", 1), ("y", -1))
 
 
@@ -32,16 +35,220 @@
     return "y" if axis == "x" else "x"
 
 
-def sum_kernel(x_ref, post_ref, out_ref, images, partial, got1, got2, in_sem, send1, recv1, send2, recv2):
-    torus = Torus()
-    per_chunk = x_ref.shape[0] // (len(ROUTES) * CHUNKS)
+def partial_scores(x_ref, r_ref, noise_ref, images, scores, raw_x, raw_r, weighted, x_sem, r_sem):
+    particles, groups, _ = x_ref.shape
+    orients = r_ref.shape[0]
+    tile = raw_x.shape[2]
+    tiles = groups // tile
+    over_lanes = (((1,), (1,)), ((), ()))
+
+    def fetch(ref, raw, sem, t):
+        slot = lax.rem(t, 2)
+        groups_of = pl.ds(pl.multiple_of(t * tile, tile), tile)
+        return pltpu.make_async_copy(ref.at[:, groups_of], raw.at[slot], sem.at[slot])
+
+    def start(t):
+        fetch(x_ref, raw_x, x_sem, t).start()
+        fetch(r_ref, raw_r, r_sem, t).start()
+
+    start(0)
+    start(1)
+    scores[...] = jnp.zeros_like(scores)
+
+    @pl.loop(0, tiles)
+    def _(t):
+        slot = lax.rem(t, 2)
+        first = t * tile
+        fetch(x_ref, raw_x, x_sem, t).wait()
+
+        @pl.loop(0, particles // ROWS)
+        def _(b):
+            span = pl.ds(pl.multiple_of(b * ROWS, ROWS), ROWS)
+            images[pl.ds(first, tile), span] = jnp.swapaxes(raw_x[slot, span], 0, 1)
+
+        fetch(r_ref, raw_r, r_sem, t).wait()
+
+        @pl.loop(0, orients // ROWS)
+        def _(b):
+            span = pl.ds(pl.multiple_of(b * ROWS, ROWS), ROWS)
+            value = jnp.swapaxes(raw_r[slot, span], 0, 1)
+            for g in range(tile):
+                scaled = value[g].astype(jnp.float32) * noise_ref[first + g]
+                weighted[g, span] = scaled.astype(jnp.bfloat16)
+
+        @pl.when(t + 2 < tiles)
+        def _():
+            start(t + 2)
+
+        for m in range(0, particles, BAND):
+            acc = scores[m : m + BAND]
+            for g in range(tile):
+                acc = acc + lax.dot_general(
+                    images[first + g, m : m + BAND], weighted[g], over_lanes,
+                    preferred_element_type=jnp.float32,
+                )
+            scores[m : m + BAND] = acc
+
+
+def slot_tables(dest_ref, row_ref, part_ref, me, counts, rows_at, parts_at, row_out, part_out):
+    slabs = lax.axis_size("slab")
+    orients = dest_ref.shape[1]
+    groups = dest_ref.shape[0] // slabs
+    doms = row_out.shape[0]
+    shift = (orients // doms).bit_length() - 1
+    here = lax.broadcasted_iota(jnp.int32, (orients, orients), 0)
+    there = lax.broadcasted_iota(jnp.int32, (orients, orients), 1)
+    same = lax.shift_right_logical(here, shift) == lax.shift_right_logical(there, shift)
+    share = same.astype(jnp.float32).astype(jnp.bfloat16)
+    before = jnp.where(same & (here < there), 1.0, 0.0).astype(jnp.bfloat16)
+    mask = (dest_ref[...] == me).astype(jnp.float32).astype(jnp.bfloat16)
+    counts[0] = jnp.dot(mask, before, preferred_element_type=jnp.float32)
+    counts[1] = jnp.dot(mask, share, preferred_element_type=jnp.float32)
+    lower = lax.broadcasted_iota(jnp.int32, (groups, groups), 0) > lax.broadcasted_iota(
+        jnp.int32, (groups, groups), 1
+    )
+    lower = lower.astype(jnp.float32).astype(jnp.bfloat16)
+
+    @pl.loop(0, slabs)
+    def _(s):
+        span = pl.ds(pl.multiple_of(s * groups, groups), groups)
+        above = jnp.dot(
+            lower, counts[1, span].astype(jnp.bfloat16), preferred_element_type=jnp.float32
+        )
+        rank = jnp.where(dest_ref[span] == me, counts[0, span] + above, -1.0)
+        row = row_ref[span].astype(jnp.float32) + 1.0
+        part = part_ref[span]
+        found_rows = []
+        found_parts = []
+        for j in range(CAP):
+            chosen = rank == j
+            found_rows.append(jnp.sum(jnp.where(chosen, row, 0.0), axis=0, keepdims=True))
+            found_parts.append(jnp.sum(jnp.where(chosen, part, 0.0), axis=0, keepdims=True))
+        slots = pl.ds(pl.multiple_of(s * CAP, CAP), CAP)
+        rows_at[slots] = jnp.concatenate(found_rows, axis=0)
+        parts_at[slots] = jnp.concatenate(found_parts, axis=0)
+
+    owner = lax.shift_right_logical(lax.broadcasted_iota(jnp.int32, (doms, orients), 1), shift)
+    gather = (owner == lax.broadcasted_iota(jnp.int32, (doms, orients), 0)).astype(jnp.float32)
+    over_lanes = (((1,), (1,)), ((), ()))
+    for found, out in ((rows_at, row_out), (parts_at, part_out)):
+        out[...] = lax.dot_general(
+            gather, found[...], over_lanes,
+            precision=lax.Precision.HIGHEST, preferred_element_type=jnp.float32,
+        )
+    row_out[...] = row_out[...] - 1.0
+
+
+class Column:
+    def __init__(self):
+        self.dom = lax.axis_index("dom")
+        self.slab = lax.axis_index("slab")
+        self.slabs = lax.axis_size("slab")
+        self.chips = self.slabs // 2
+        self.chip = lax.div(self.slab, 2)
+        self.core = lax.rem(self.slab, 2)
+        self.mate = (self.dom, 2 * self.chip + 1 - self.core)
+
+    def peer(self, step):
+        return (self.dom, 2 * lax.rem(self.chip + step, self.chips) + self.core)
+
+
+def posteriors(
+    column, scores_ref, blocks_ref, post_ref, meanwhile,
+    mine, from_mate, total, from_chips, found,
+    mate_send, mate_recv, chip_send, chip_recv, back_send, back_recv, last_send, last_recv,
+):
+    slabs, chips, chip, core = column.slabs, column.chips, column.chip, column.core
+    mate, peer = column.mate, column.peer
+    count = mine.shape[2]
+
+    def picked(span, which):
+        chosen = blocks_ref[span, which : which + 1]
+        value = scores_ref[span, 0:OB]
+        for b in range(1, scores_ref.shape[1] // OB):
+            value = jnp.where(chosen == b, scores_ref[span, b * OB : (b + 1) * OB], value)
+        return value
+
+    for s in range(slabs):
+        span = pl.ds(s * count, count)
+        for which in range(2):
+            mine[s % 2, s // 2, :, which * OB : (which + 1) * OB] = picked(span, which)
+    to_mate = pltpu.make_async_remote_copy(
+        src_ref=mine.at[1 - core],
+        dst_ref=from_mate,
+        send_sem=mate_send,
+        recv_sem=mate_recv,
+        device_id=mate,
+        device_id_type=MESH,
+    )
+    to_mate.start()
+    to_mate.wait_recv()
+    total[...] = mine[core] + from_mate[...]
+
+    def to_chip(step):
+        return pltpu.make_async_remote_copy(
+            src_ref=total.at[lax.rem(chip + step, chips)],
+            dst_ref=from_chips.at[step - 1],
+            send_sem=chip_send.at[step - 1],
+            recv_sem=chip_recv.at[step - 1],
+            device_id=peer(step),
+            device_id_type=MESH,
+        )
+
+    for step in range(1, chips):
+        to_chip(step).start()
+    meanwhile()
+    for step in range(1, chips):
+        to_chip(step).wait_recv()
+    scores = total[chip]
+    for step in range(1, chips):
+        scores = scores + from_chips[step - 1]
+    weights = jnp.exp(scores - jnp.max(scores, axis=1, keepdims=True))
+    found[chip, core] = (weights / jnp.sum(weights, axis=1, keepdims=True)).astype(jnp.bfloat16)
+
+    def back(step):
+        return pltpu.make_async_remote_copy(
+            src_ref=found.at[chip, core],
+            dst_ref=found.at[chip, core],
+            send_sem=back_send.at[step - 1],
+            recv_sem=back_recv.at[step - 1],
+            device_id=peer(step),
+            device_id_type=MESH,
+        )
+
+    for step in range(1, chips):
+        back(step).start()
+    for step in range(1, chips):
+        back(step).wait_recv()
+    last = pltpu.make_async_remote_copy(
+        src_ref=found.at[:, core],
+        dst_ref=found.at[:, core],
+        send_sem=last_send,
+        recv_sem=last_recv,
+        device_id=mate,
+        device_id_type=MESH,
+    )
+    last.start()
+    last.wait_recv()
+    everyone = found[...].astype(jnp.float32).reshape(slabs * count, 2 * OB)
+    first, second = blocks_ref[:, 0:1], blocks_ref[:, 1:2]
+    for b in range(scores_ref.shape[1] // OB):
+        value = jnp.where(first == b, everyone[:, :OB], 0.0)
+        value = jnp.where(second == b, everyone[:, OB:], value)
+        post_ref[b * OB : (b + 1) * OB, :] = value.T.astype(jnp.bfloat16)
+    to_mate.wait_send()
+    last.wait_send()
+    for step in range(1, chips):
+        to_chip(step).wait_send()
+        back(step).wait_send()
+
+
+def sum_over_dom(torus, images, post_ref, out_ref, partial, got1, got2, send1, recv1, send2, recv2):
+    per_chunk = images.shape[0] // (len(ROUTES) * CHUNKS)
     share = out_ref.shape[1]
 
-    def fetch(q, i):
-        first = (q * CHUNKS + i) * per_chunk
-        return pltpu.make_async_copy(
-            x_ref.at[pl.ds(first, per_chunk)], images.at[q, i], in_sem.at[q, i]
-        )
+    def first_group(q, i):
+        return (i * len(ROUTES) + q) * per_chunk
 
     def block(q, stage, hop):
         axis, sign = ROUTES[q]
@@ -76,23 +283,13 @@
         return (a.astype(jnp.float32) + b.astype(jnp.float32)).astype(jnp.bfloat16)
 
     routes = range(len(ROUTES))
-    for i in range(CHUNKS):
-        for q in routes:
-            fetch(q, i).start()
-    barrier = pltpu.get_barrier_semaphore()
-    for axis, sign in ROUTES:
-        pl.semaphore_signal(
-            barrier, inc=1, device_id=torus.neighbour(axis, sign), device_id_type=MESH
-        )
-    pl.semaphore_wait(barrier, len(ROUTES))
 
     @pl.loop(0, CHUNKS)
     def _(i):
         for q in routes:
-            fetch(q, i).wait()
             for j in range(per_chunk):
                 value = jnp.dot(
-                    post_ref[...], images[q, i, j], preferred_element_type=jnp.float32
+                    post_ref[...], images[first_group(q, i) + j], preferred_element_type=jnp.float32
                 ).astype(jnp.bfloat16)
                 for yy in range(SIDE):
                     for xx in range(SIDE):
@@ -133,8 +330,7 @@
         for q in routes:
             hop2(q, last, i).wait_recv()
             mine = got1[q, last, i, torus.at[other(ROUTES[q][0])]]
-            first = (q * CHUNKS + i) * per_chunk
-            out_ref[pl.ds(first, per_chunk)] = added(got2[q, last, i], mine)
+            out_ref[pl.ds(first_group(q, i), per_chunk)] = added(got2[q, last, i], mine)
 
     @pl.loop(0, CHUNKS)
     def _(i):
@@ -144,38 +340,87 @@
                 hop2(q, hop, i).wait_send()
 
 
-def summed_slices(images, posterior, share):
-    groups, particles, width = images.shape
-    orients = posterior.shape[0]
+def project_kernel(
+    x_ref, r_ref, noise_ref, blocks_ref, dest_ref, row_ref, part_ref,
+    out_ref, row_out, part_out,
+    images, scores, raw_x, raw_r, weighted, post, *rest
+):
+    x_sem, r_sem = rest[:2]
+    post_scratch = rest[2:7]
+    counts, rows_at, parts_at = rest[7:10]
+    post_sems = rest[10:18]
+    sum_scratch = rest[18:]
+    torus = Torus()
+    column = Column()
+    me = column.dom * column.slabs + column.slab
+    barrier = pltpu.get_barrier_semaphore()
+    others = [column.mate] + [column.peer(step) for step in range(1, column.chips)]
+    others = others + [torus.neighbour(axis, sign) for axis, sign in ROUTES]
+    for device in others:
+        pl.semaphore_signal(barrier, inc=1, device_id=device, device_id_type=MESH)
+    partial_scores(x_ref, r_ref, noise_ref, images, scores, raw_x, raw_r, weighted, x_sem, r_sem)
+    pl.semaphore_wait(barrier, len(others))
+
+    def meanwhile():
+        slot_tables(dest_ref, row_ref, part_ref, me, counts, rows_at, parts_at, row_out, part_out)
+
+    posteriors(column, scores, blocks_ref, post, meanwhile, *post_scratch, *post_sems)
+    sum_over_dom(torus, images, post, out_ref, *sum_scratch)
+
+
+def summed_slices(particles, references, inv_noise, blocks, destination, row_index, fraction, doms, slabs):
+    count, groups, width = particles.shape
+    orients = references.shape[0]
+    share = orients // doms
+    chips = slabs // 2
+    part = count // slabs
     routes = len(ROUTES)
-    per_chunk = groups // (routes * CHUNKS)
     hops = SIDE - 1
-    piece = (per_chunk, share, width)
-    sems = pltpu.SemaphoreType.DMA((routes, hops, CHUNKS))
+    piece = (groups // (routes * CHUNKS), share, width)
+    vmem = pl.BlockSpec(memory_space=pltpu.VMEM)
+    hbm = pl.BlockSpec(memory_space=pl.ANY)
+    dma = pltpu.SemaphoreType.DMA
+    table = jax.ShapeDtypeStruct((doms, slabs * CAP), jnp.float32)
     return pl.pallas_call(
-        sum_kernel,
-        out_shape=jax.ShapeDtypeStruct((groups, share, width), jnp.bfloat16),
-        in_specs=[
-            pl.BlockSpec(memory_space=pl.ANY),
-            pl.BlockSpec(memory_space=pltpu.VMEM),
-        ],
-        out_specs=pl.BlockSpec(memory_space=pltpu.VMEM),
+        project_kernel,
+        out_shape=(jax.ShapeDtypeStruct((groups, share, width), jnp.bfloat16), table, table),
+        in_specs=[hbm, hbm, pl.BlockSpec(memory_space=pltpu.SMEM)] + [vmem] * 4,
+        out_specs=(vmem,) * 3,
         scratch_shapes=[
-            pltpu.VMEM((routes, CHUNKS, per_chunk, particles, width), jnp.bfloat16),
+            pltpu.VMEM((groups, count, width), jnp.bfloat16),
+            pltpu.VMEM((count, orients), jnp.float32),
+            pltpu.VMEM((2, count, TILE, width), jnp.bfloat16),
+            pltpu.VMEM((2, orients, TILE, width), jnp.bfloat16),
+            pltpu.VMEM((TILE, orients, width), jnp.bfloat16),
+            pltpu.VMEM((orients, count), jnp.bfloat16),
+            dma((2,)),
+            dma((2,)),
+            pltpu.VMEM((2, chips, part, 2 * OB), jnp.float32),
+            pltpu.VMEM((chips, part, 2 * OB), jnp.float32),
+            pltpu.VMEM((chips, part, 2 * OB), jnp.float32),
+            pltpu.VMEM((chips - 1, part, 2 * OB), jnp.float32),
+            pltpu.VMEM((chips, 2, part, 2 * OB), jnp.bfloat16),
+            pltpu.VMEM((2,) + destination.shape, jnp.float32),
+            pltpu.VMEM((slabs * CAP, orients), jnp.float32),
+            pltpu.VMEM((slabs * CAP, orients), jnp.float32),
+            dma,
+            dma,
+            dma((chips - 1,)),
+            dma((chips - 1,)),
+            dma((chips - 1,)),
+            dma((chips - 1,)),
+            dma,
+            dma,
             pltpu.VMEM((routes, CHUNKS, SIDE, SIDE) + piece, jnp.bfloat16),
             pltpu.VMEM((routes, hops, CHUNKS, SIDE) + piece, jnp.bfloat16),
             pltpu.VMEM((routes, hops, CHUNKS) + piece, jnp.bfloat16),
-            pltpu.SemaphoreType.DMA((routes, CHUNKS)),
-            sems,
-            sems,
-            sems,
-            sems,
-        ],
+        ]
+        + [dma((routes, hops, CHUNKS))] * 4,
         compiler_params=pltpu.CompilerParams(
-            collective_id=0, has_side_effects=True, vmem_limit_bytes=48 * 1024 * 1024
+            collective_id=0, has_side_effects=True, vmem_limit_bytes=58 * 1024 * 1024
         ),
-        name="sum_slices",
-    )(images, posterior)
+        name="project",
+    )(particles, references, inv_noise, blocks, destination, row_index, fraction)
 
 
 def exchange_kernel(
@@ -223,7 +468,7 @@
     own = pltpu.make_async_copy(packed.at[me], got.at[me], own_sem)
     own.start()
     lanes = row_ref.shape[1]
-    rows = lax.broadcasted_iota(jnp.int32, (RD, lanes), 0)
+    rows = lax.broadcasted_iota(jnp.int32, (RD, lanes), 0).astype(jnp.float32)
     for b in range(row_ref.shape[0]):
         row = row_ref[b : b + 1, :]
         part = part_ref[b : b + 1, :]
@@ -348,62 +593,25 @@
     return dests * CAP + rank
 
 
-def received_slots(tables, dests, me):
-    count = dests.shape[1]
-    mask = dests == me
-    place = jnp.arange(count, dtype=jnp.int32)
-    before = (place[:, None] < place[None, :]).astype(jnp.bfloat16)
-    rank = jnp.dot(mask.astype(jnp.bfloat16), before, preferred_element_type=jnp.float32)
-    rank = jnp.where(mask, rank.astype(jnp.int32), -1)
-    chosen = rank[:, None, :] == jnp.arange(CAP, dtype=jnp.int32)[None, :, None]
-    found = [jnp.sum(jnp.where(chosen, t[:, None, :], 0), axis=2).reshape(-1) for t in tables]
-    filled = jnp.any(chosen, axis=2).reshape(-1)
-    return found, filled
-
-
 def shards(particles, blocks, references, inv_noise, destination, row_index, fraction):
-    particle_count, groups, row_width = particles.shape
+    _, groups, row_width = particles.shape
     orients = references.shape[0]
     dom_size = lax.axis_size("dom")
     slab_size = lax.axis_size("slab")
     devices = dom_size * slab_size
     dom_pos = lax.axis_index("dom")
     slab_pos = lax.axis_index("slab")
-    me = dom_pos * slab_size + slab_pos
     share = orients // dom_size
-    weighted = (references.astype(jnp.float32) * inv_noise[None, :, None]).astype(jnp.bfloat16)
-    partial_value = lax.dot_general(
-        weighted, particles, (((1, 2), (1, 2)), ((), ())), preferred_element_type=jnp.float32
+    pieces, row, part = summed_slices(
+        particles, references, inv_noise, blocks, destination, row_index, fraction, dom_size, slab_size
     )
-    scores = lax.psum(partial_value, "slab")
-    block_of = jnp.arange(orients, dtype=jnp.int32) // OB
-    allowed = jnp.any(blocks.T[:, None, :] == block_of[None, :, None], axis=0)
-    masked = jnp.where(allowed, scores, -jnp.inf)
-    highest = jnp.max(masked, axis=0, keepdims=True)
-    weights = jnp.where(allowed, jnp.exp(masked - highest), 0.0)
-    posterior = (weights / jnp.sum(weights, axis=0, keepdims=True)).astype(jnp.bfloat16)
-    pieces = summed_slices(particles.transpose(1, 0, 2), posterior, share)
     pieces = pieces.reshape(groups * share, row_width)
 
     my_dest = lax.dynamic_slice(
         destination, (slab_pos * groups, dom_pos * share), (groups, share)
     )
     slot = send_slots(my_dest.reshape(-1), devices)
-    def by_source(table):
-        table = table.reshape(slab_size, groups, dom_size, share).transpose(2, 0, 1, 3)
-        return table.reshape(devices, share * groups)
-
-    (row, part), filled = received_slots(
-        (by_source(row_index), by_source(fraction)), by_source(destination), me
-    )
-    row = jnp.where(filled, row, -2)
-    volume, next_slab = exchanged(
-        pieces,
-        slot[None, :],
-        row.reshape(dom_size, -1),
-        part.reshape(dom_size, -1),
-        devices,
-    )
+    volume, next_slab = exchanged(pieces, slot[None, :], row, part, devices)
     next_slab = next_slab.reshape(dom_size * RD, row_width)
     return (volume, next_slab)
 

time: 224 us -> 151 us (0.67)
  Pallas kernels: 110 us -> 143 us
  waiting for transfers between devices: 27.5 us -> 0 us
  local copies, waits for them, and re-layouts: 30 us -> 5.52 us
  other arithmetic: 23.5 us -> 0.82 us
  matrix products: 18.3 us -> 0.93 us
  between operations: 14.2 us -> 0.7 us
    pallas_call x1, Pallas kernels: 63.1 us -> 95.9 us  [summed_slices(): pl.pallas_call(project_kernel, out_shape=(jax.ShapeDtypeStruct((groups, s...]
    psum x1 -> x0, waiting for transfers between devices: 27.5 us -> none  [shards(): scores = lax.psum(partial_value, 'slab')]
    dot_general x2 -> x0, matrix products: 17.4 us -> none  [the longest x1 16.8 us: shards(): lax.dot_general(weighted, particles, (((1, 2), (1, 2)), ((), ())), prefer...]
    convert_element_type x2 -> x0, other arithmetic: 12.1 us -> none  [the longest x1 10.6 us: shards(): (references.astype(jnp.float32) * inv_noise[None, :, None]).astype(jnp.bf...]
    unnamed x11, local copies, waits for them, and re-layouts: 14.2 us -> 5.36 us
    reduce_sum x3 -> x0, other arithmetic: 7.22 us -> none  [the longest x2 5.69 us: received_slots(): jnp.sum(jnp.where(chosen, t[:, None, :], 0), axis=2).reshape(-1)]
    transpose x2 -> x0, local copies, waits for them, and re-layouts: 4.48 us -> none  [by_source(): table.reshape(slab_size, groups, dom_size, share).transpose(2, 0, 1, 3)]
    reshape x2 -> x0, local copies, waits for them, and re-layouts: 4.25 us -> none  [by_source(): table.reshape(slab_size, groups, dom_size, share).transpose(2, 0, 1, 3)]
  transfers between devices with their start and end apart: 1 -> 0, of which waited for: 1 -> 0; matrix products, arithmetic and copies ran while one was open for 17% -> 0% of each run, Pallas kernels for 0% -> 0%
where the time goes in v5:
time: 151 us
  Pallas kernels  143 us (95%)
  local copies, waits for them, and re-layouts  5.52 us (4%)
    pallas_call x1, Pallas kernels, summed_slices(): pl.pallas_call(project_kernel, out_shape=(jax.ShapeDtypeStruct((groups, s...  95.9 us
    pallas_call x1, Pallas kernels, exchanged(): pl.pallas_call(exchange_kernel, out_shape=(jax.ShapeDtypeStruct((RD, widt...  46.8 us
    unnamed x11, local copies, waits for them, and re-layouts  5.36 us

profile of v5, /device:TPU:0, one launch (start us, length us, event | category | flops | bytes accessed | tf_op | source)
XLA Modules:
  0.0 150.7 jit_solution(4993540814355838892)
XLA Ops:
  0.6 0.0 copy-start.3
  0.6 0.8 broadcast_multiply_fusion
  1.5 0.1 mul.26
  1.5 0.1 eq.15
  1.6 0.9 fusion.2
  2.6 0.0 copy-done.3
  2.6 0.9 copy.10.blocks_ref
  3.5 95.9 %project.1 = (bf16[40,32,256]{2,1,0:T(8,128)(2,1)}, f32[16,128]{1,0:T(8,128)}, f32[16,128]{1,0:T(8,128)}) custom-call(bf16[512,40,256]{2,1,0:T(8,128)(2,1)} %x_ref.1, bf16[512,40,256]{2,1,0:T(8,128)(2,1)} %r_ref.1, f32[40]{0:T(128)} %noise_ref.1, s32[512,2]{1,0:T(8,128)} %copy.10.blocks_ref, s32[320,512]{1,0:T(8,128)} %dest_ref.1, s32[320,512]{1,0:T(8,128)} %row_ref.1, ...), custom_call_target="tpu_custom_call" | custom-call | tf_op jit(solution)/shard_map/project/pallas_call | solution.py:384
  99.4 0.0 copy-start
  99.4 1.1 copy-done
  100.4 0.0 copy-start.1
  100.4 0.7 copy-done.1
  101.1 0.0 copy-start.2
  101.1 0.7 copy-done.2
  101.8 46.8 %exchange_pieces.1 = (f32[256,256]{1,0:T(8,128)S(1)}, bf16[4,4,4,64,256]{4,3,2,1,0:T(8,128)(2,1)S(1)}) custom-call(bf16[1280,256]{1,0:T(8,128)(2,1)S(1)} %bitcast.3, s32[1,1280]{1,0:T(1,128)S(1)} %reshape_add_fusion.slot_ref, f32[16,128]{1,0:T(8,128)S(1)} %copy-done.1, f32[16,128]{1,0:T(8,128)S(1)} %copy-done.2), custom_call_target="tpu_custom_call" | custom-call | tf_op jit(solution)/shard_map/exchange_pieces/pallas_call | solution.py:559
  148.6 0.7 copy.13
  149.3 1.3 copy.14
  (2 shorter events, 0.0 us)
Async XLA Ops:
  0.6 2.0 %copy-start.3 = (s32[512,2]{0,1:T(2,128)S(1)}, s32[512,2]{0,1:T(2,128)}, u32[]{:S(2)}) copy-start(s32[512,2]{0,1:T(2,128)} %param.8) | copy-start | bytes 12292
  99.4 1.1 copy-start
  100.4 0.7 copy-start.1
  101.1 0.7 copy-start.2

commit v6 on v5

--- a/solution.py
+++ b/solution.py
@@ -154,7 +154,7 @@
 
 
 def posteriors(
-    column, scores_ref, blocks_ref, post_ref, meanwhile,
+    column, scores_ref, chosen_ref, post_ref, meanwhile, afterwards,
     mine, from_mate, total, from_chips, found,
     mate_send, mate_recv, chip_send, chip_recv, back_send, back_recv, last_send, last_recv,
 ):
@@ -163,7 +163,7 @@
     count = mine.shape[2]
 
     def picked(span, which):
-        chosen = blocks_ref[span, which : which + 1]
+        chosen = chosen_ref[span, SIDE * which : SIDE * which + 1]
         value = scores_ref[span, 0:OB]
         for b in range(1, scores_ref.shape[1] // OB):
             value = jnp.where(chosen == b, scores_ref[span, b * OB : (b + 1) * OB], value)
@@ -218,6 +218,7 @@
 
     for step in range(1, chips):
         back(step).start()
+    afterwards()
     for step in range(1, chips):
         back(step).wait_recv()
     last = pltpu.make_async_remote_copy(
@@ -231,7 +232,7 @@
     last.start()
     last.wait_recv()
     everyone = found[...].astype(jnp.float32).reshape(slabs * count, 2 * OB)
-    first, second = blocks_ref[:, 0:1], blocks_ref[:, 1:2]
+    first, second = chosen_ref[:, 0:1], chosen_ref[:, SIDE : SIDE + 1]
     for b in range(scores_ref.shape[1] // OB):
         value = jnp.where(first == b, everyone[:, :OB], 0.0)
         value = jnp.where(second == b, everyone[:, OB:], value)
@@ -340,16 +341,163 @@
                 hop2(q, hop, i).wait_send()
 
 
+def insertion_weights(row_ref, part_ref, insert):
+    lanes = row_ref.shape[1]
+    rows = lax.broadcasted_iota(jnp.int32, (RD, lanes), 0).astype(jnp.float32)
+    for b in range(row_ref.shape[0]):
+        row = row_ref[b : b + 1, :]
+        part = part_ref[b : b + 1, :]
+        weight = jnp.where(rows == row, 1.0 - part, 0.0) + jnp.where(rows == row + 1, part, 0.0)
+        high = weight.astype(jnp.bfloat16)
+        insert[0, :, b * lanes : (b + 1) * lanes] = high
+        insert[1, :, b * lanes : (b + 1) * lanes] = (weight - high.astype(jnp.float32)).astype(jnp.bfloat16)
+
+
+def insert_pieces(torus, pieces_ref, slot_ref, insert, volume_ref, packed, got, own_sem, out_sem, in_sem):
+    slabs = lax.axis_size("slab")
+    devices = lax.axis_size("dom") * slabs
+    me = (torus.at["y"] * SIDE + torus.at["x"]) * slabs + torus.slab
+    width = pieces_ref.shape[2]
+    count = pieces_ref.shape[0] * pieces_ref.shape[1]
+    block = RD
+    owners = block // CAP
+    numbers = lax.broadcasted_iota(jnp.int32, (block, count), 0)
+    pieces = pieces_ref[...].reshape(count, width)
+
+    @pl.loop(0, devices // owners)
+    def _(k):
+        b = lax.rem(lax.div(me, owners) + k, devices // owners)
+        first = b * owners
+        pick = (numbers + b * block == slot_ref[...]).astype(jnp.float32).astype(jnp.bfloat16)
+        value = jnp.dot(pick, pieces, preferred_element_type=jnp.float32)
+        packed[pl.ds(first, owners)] = value.astype(jnp.bfloat16).reshape(owners, CAP, width)
+
+        @pl.loop(0, owners)
+        def _(j):
+            to = first + lax.rem(me + j, owners)
+
+            @pl.when(to != me)
+            def _():
+                pltpu.make_async_remote_copy(
+                    src_ref=packed.at[to],
+                    dst_ref=got.at[me],
+                    send_sem=out_sem,
+                    recv_sem=in_sem,
+                    device_id=(lax.div(to, slabs), lax.rem(to, slabs)),
+                    device_id_type=MESH,
+                ).start()
+
+    own = pltpu.make_async_copy(packed.at[me], got.at[me], own_sem)
+    own.start()
+    own.wait()
+    others = got.at[pl.ds(0, devices - 1)]
+    pltpu.make_async_copy(others, others, in_sem).wait()
+    received = got[...].reshape(devices * CAP, width)
+    volume = jnp.dot(insert[0], received, preferred_element_type=jnp.float32)
+    volume_ref[...] = volume + jnp.dot(insert[1], received, preferred_element_type=jnp.float32)
+    sent = packed.at[pl.ds(0, devices - 1)]
+    return pltpu.make_async_copy(sent, sent, out_sem)
+
+
+def gather_rows(torus, volume_ref, next_ref, send_a, recv_a, send_b, recv_b):
+    axes = ("x", "y")
+    steps = (1, -1)
+    rows = next_ref.shape[4]
+    for c in range(2):
+        for half in range(2):
+            first = (2 * c + half) * rows
+            next_ref[torus.at["y"], torus.at["x"], c, half] = volume_ref[
+                first : first + rows
+            ].astype(jnp.bfloat16)
+
+    def spot(c, back1, back2, half=None):
+        along = lax.rem(torus.at[axes[c]] + back1 + SIDE, SIDE)
+        across = lax.rem(torus.at[axes[1 - c]] + back2 + SIDE, SIDE)
+        y, x = (across, along) if c == 0 else (along, across)
+        return next_ref.at[y, x, c] if half is None else next_ref.at[y, x, c, half]
+
+    def copy(where, axis, step, send, recv):
+        return pltpu.make_async_remote_copy(
+            src_ref=where,
+            dst_ref=where,
+            send_sem=send,
+            recv_sem=recv,
+            device_id=torus.neighbour(axis, step),
+            device_id_type=MESH,
+        )
+
+    def first_a(c, way):
+        return copy(spot(c, 0, 0), axes[c], steps[way], send_a.at[0, c, way], recv_a.at[0, c, way])
+
+    def second_a(c, way):
+        where = spot(c, -steps[way], 0, way)
+        return copy(where, axes[c], steps[way], send_a.at[1, c, way], recv_a.at[1, c, way])
+
+    def first_b(c, j, way):
+        where = spot(c, (0, -1, 1, 2)[j], 0)
+        return copy(
+            where, axes[1 - c], steps[way], send_b.at[0, c, j, way], recv_b.at[0, c, j, way]
+        )
+
+    def second_b(c, j, way):
+        where = spot(c, (0, -1, 1, 2)[j], -steps[way], way)
+        return copy(
+            where, axes[1 - c], steps[way], send_b.at[1, c, j, way], recv_b.at[1, c, j, way]
+        )
+
+    both = range(2)
+    for c in both:
+        for way in both:
+            first_a(c, way).start()
+    for c in both:
+        for way in both:
+            first_b(c, 0, way).start()
+    for way in both:
+        for c in both:
+            first_a(c, way).wait_recv()
+            second_a(c, way).start()
+            for out in both:
+                first_b(c, 1 + way, out).start()
+
+    def forward(j):
+        for c in both:
+            for way in both:
+                first_b(c, j, way).wait_recv()
+                second_b(c, j, way).start()
+
+    forward(0)
+    for c in both:
+        for way in both:
+            second_a(c, way).wait_recv()
+        for out in both:
+            first_b(c, 3, out).start()
+    for j in range(1, SIDE):
+        forward(j)
+    for j in range(SIDE):
+        for c in both:
+            for way in both:
+                second_b(c, j, way).wait_recv()
+    for c in both:
+        for way in both:
+            first_a(c, way).wait_send()
+            second_a(c, way).wait_send()
+            for j in range(SIDE):
+                first_b(c, j, way).wait_send()
+                second_b(c, j, way).wait_send()
+
+
 def project_kernel(
-    x_ref, r_ref, noise_ref, blocks_ref, dest_ref, row_ref, part_ref,
-    out_ref, row_out, part_out,
-    images, scores, raw_x, raw_r, weighted, post, *rest
+    x_ref, r_ref, noise_ref, blocks_ref, dest_ref, row_ref, part_ref, slot_ref,
+    volume_ref, next_ref,
+    images, scores, raw_x, raw_r, weighted, post, chosen, row_at, part_at, insert, pieces, *rest
 ):
     x_sem, r_sem = rest[:2]
     post_scratch = rest[2:7]
     counts, rows_at, parts_at = rest[7:10]
     post_sems = rest[10:18]
-    sum_scratch = rest[18:]
+    sum_scratch = rest[18:25]
+    insert_scratch = rest[25:30]
+    gather_sems = rest[30:]
     torus = Torus()
     column = Column()
     me = column.dom * column.slabs + column.slab
@@ -358,34 +506,48 @@
     others = others + [torus.neighbour(axis, sign) for axis, sign in ROUTES]
     for device in others:
         pl.semaphore_signal(barrier, inc=1, device_id=device, device_id_type=MESH)
+    both = blocks_ref[...].astype(jnp.float32)
+    half = chosen.shape[1] // 2
+    both = jnp.concatenate([both[0:1]] * half + [both[1:2]] * half, axis=0)
+    chosen[...] = both.T
     partial_scores(x_ref, r_ref, noise_ref, images, scores, raw_x, raw_r, weighted, x_sem, r_sem)
     pl.semaphore_wait(barrier, len(others))
 
-    def meanwhile():
-        slot_tables(dest_ref, row_ref, part_ref, me, counts, rows_at, parts_at, row_out, part_out)
-
-    posteriors(column, scores, blocks_ref, post, meanwhile, *post_scratch, *post_sems)
-    sum_over_dom(torus, images, post, out_ref, *sum_scratch)
-
-
-def summed_slices(particles, references, inv_noise, blocks, destination, row_index, fraction, doms, slabs):
+    def tables():
+        slot_tables(dest_ref, row_ref, part_ref, me, counts, rows_at, parts_at, row_at, part_at)
+
+    def weights():
+        insertion_weights(row_at, part_at, insert)
+
+    posteriors(column, scores, chosen, post, tables, weights, *post_scratch, *post_sems)
+    sum_over_dom(torus, images, post, pieces, *sum_scratch)
+    sent = insert_pieces(torus, pieces, slot_ref, insert, volume_ref, *insert_scratch)
+    gather_rows(torus, volume_ref, next_ref, *gather_sems)
+    sent.wait()
+
+
+def project(particles, references, inv_noise, blocks, destination, row_index, fraction, slot, doms, slabs):
     count, groups, width = particles.shape
     orients = references.shape[0]
     share = orients // doms
     chips = slabs // 2
     part = count // slabs
+    devices = doms * slabs
     routes = len(ROUTES)
     hops = SIDE - 1
     piece = (groups // (routes * CHUNKS), share, width)
     vmem = pl.BlockSpec(memory_space=pltpu.VMEM)
     hbm = pl.BlockSpec(memory_space=pl.ANY)
     dma = pltpu.SemaphoreType.DMA
-    table = jax.ShapeDtypeStruct((doms, slabs * CAP), jnp.float32)
+    table = pltpu.VMEM((doms, slabs * CAP), jnp.float32)
     return pl.pallas_call(
         project_kernel,
-        out_shape=(jax.ShapeDtypeStruct((groups, share, width), jnp.bfloat16), table, table),
-        in_specs=[hbm, hbm, pl.BlockSpec(memory_space=pltpu.SMEM)] + [vmem] * 4,
-        out_specs=(vmem,) * 3,
+        out_shape=(
+            jax.ShapeDtypeStruct((RD, width), jnp.float32),
+            jax.ShapeDtypeStruct((SIDE, SIDE, 2, 2, RD // 4, width), jnp.bfloat16),
+        ),
+        in_specs=[hbm, hbm, pl.BlockSpec(memory_space=pltpu.SMEM)] + [vmem] * 5,
+        out_specs=(vmem, vmem),
         scratch_shapes=[
             pltpu.VMEM((groups, count, width), jnp.bfloat16),
             pltpu.VMEM((count, orients), jnp.float32),
@@ -393,6 +555,11 @@
             pltpu.VMEM((2, orients, TILE, width), jnp.bfloat16),
             pltpu.VMEM((TILE, orients, width), jnp.bfloat16),
             pltpu.VMEM((orients, count), jnp.bfloat16),
+            pltpu.VMEM((count, 8), jnp.float32),
+            table,
+            table,
+            pltpu.VMEM((2, RD, devices * CAP), jnp.bfloat16),
+            pltpu.VMEM((groups, share, width), jnp.bfloat16),
             dma((2,)),
             dma((2,)),
             pltpu.VMEM((2, chips, part, 2 * OB), jnp.float32),
@@ -414,173 +581,25 @@
             pltpu.VMEM((routes, CHUNKS, SIDE, SIDE) + piece, jnp.bfloat16),
             pltpu.VMEM((routes, hops, CHUNKS, SIDE) + piece, jnp.bfloat16),
             pltpu.VMEM((routes, hops, CHUNKS) + piece, jnp.bfloat16),
-        ]
-        + [dma((routes, hops, CHUNKS))] * 4,
+            dma((routes, hops, CHUNKS)),
+            dma((routes, hops, CHUNKS)),
+            dma((routes, hops, CHUNKS)),
+            dma((routes, hops, CHUNKS)),
+            pltpu.VMEM((devices, CAP, width), jnp.bfloat16),
+            pltpu.VMEM((devices, CAP, width), jnp.bfloat16),
+            dma,
+            dma,
+            dma,
+            dma((2, 2, 2)),
+            dma((2, 2, 2)),
+            dma((2, 2, SIDE, 2)),
+            dma((2, 2, SIDE, 2)),
+        ],
         compiler_params=pltpu.CompilerParams(
-            collective_id=0, has_side_effects=True, vmem_limit_bytes=58 * 1024 * 1024
+            collective_id=0, has_side_effects=True, vmem_limit_bytes=60 * 1024 * 1024
         ),
         name="project",
-    )(particles, references, inv_noise, blocks, destination, row_index, fraction)
-
-
-def exchange_kernel(
-    pieces_ref, slot_ref, row_ref, part_ref, volume_ref, next_ref,
-    packed, got, insert, own_sem, out_sem, in_sem, send_a, recv_a, send_b, recv_b,
-):
-    torus = Torus()
-    slabs = lax.axis_size("slab")
-    devices = lax.axis_size("dom") * slabs
-    me = (torus.at["y"] * SIDE + torus.at["x"]) * slabs + torus.slab
-    width = pieces_ref.shape[1]
-    routes = range(len(ROUTES))
-
-    def device(number):
-        return (lax.div(number, slabs), lax.rem(number, slabs))
-
-    barrier = pltpu.get_barrier_semaphore()
-
-    @pl.loop(1, devices)
-    def _(k):
-        to = lax.rem(me + k, devices)
-        pl.semaphore_signal(barrier, inc=1, device_id=device(to), device_id_type=MESH)
-
-    block = RD
-    owners = block // CAP
-    numbers = lax.broadcasted_iota(jnp.int32, (block, pieces_ref.shape[0]), 0)
-    for b in range(devices // owners):
-        pick = (numbers + b * block == slot_ref[...]).astype(jnp.float32).astype(jnp.bfloat16)
-        value = jnp.dot(pick, pieces_ref[...], preferred_element_type=jnp.float32)
-        packed[b * owners : (b + 1) * owners] = value.astype(jnp.bfloat16).reshape(owners, CAP, width)
-    pl.semaphore_wait(barrier, devices - 1)
-
-    @pl.loop(1, devices)
-    def _(k):
-        to = lax.rem(me + k, devices)
-        pltpu.make_async_remote_copy(
-            src_ref=packed.at[to],
-            dst_ref=got.at[me],
-            send_sem=out_sem,
-            recv_sem=in_sem,
-            device_id=device(to),
-            device_id_type=MESH,
-        ).start()
-
-    own = pltpu.make_async_copy(packed.at[me], got.at[me], own_sem)
-    own.start()
-    lanes = row_ref.shape[1]
-    rows = lax.broadcasted_iota(jnp.int32, (RD, lanes), 0).astype(jnp.float32)
-    for b in range(row_ref.shape[0]):
-        row = row_ref[b : b + 1, :]
-        part = part_ref[b : b + 1, :]
-        weight = jnp.where(rows == row, 1.0 - part, 0.0) + jnp.where(rows == row + 1, part, 0.0)
-        high = weight.astype(jnp.bfloat16)
-        insert[0, :, b * lanes : (b + 1) * lanes] = high
-        insert[1, :, b * lanes : (b + 1) * lanes] = (weight - high.astype(jnp.float32)).astype(jnp.bfloat16)
-    own.wait()
-    others = got.at[pl.ds(0, devices - 1)]
-    pltpu.make_async_copy(others, others, in_sem).wait()
-    pieces = got[...].reshape(devices * CAP, width)
-    volume = jnp.dot(insert[0], pieces, preferred_element_type=jnp.float32)
-    volume = volume + jnp.dot(insert[1], pieces, preferred_element_type=jnp.float32)
-    volume_ref[...] = volume
-    part_rows = RD // len(ROUTES)
-    for q in routes:
-        next_ref[torus.at["y"], torus.at["x"], q] = volume[
-            q * part_rows : (q + 1) * part_rows
-        ].astype(jnp.bfloat16)
-
-    def origin(q, stage, hop):
-        axis, sign = ROUTES[q]
-        axis = axis if stage == 1 else other(axis)
-        return lax.rem(torus.at[axis] - sign * hop + 2 * SIDE, SIDE)
-
-    def place(q, first, second):
-        y, x = (second, first) if ROUTES[q][0] == "x" else (first, second)
-        return next_ref.at[y, x, q]
-
-    def hop_a(q, hop):
-        axis, sign = ROUTES[q]
-        spot = place(q, origin(q, 1, hop), torus.at[other(axis)])
-        return pltpu.make_async_remote_copy(
-            src_ref=spot,
-            dst_ref=spot,
-            send_sem=send_a.at[q, hop],
-            recv_sem=recv_a.at[q, hop],
-            device_id=torus.neighbour(axis, sign),
-            device_id_type=MESH,
-        )
-
-    def hop_b(q, hop, j):
-        axis, sign = ROUTES[q]
-        spot = place(q, origin(q, 1, j), origin(q, 2, hop))
-        return pltpu.make_async_remote_copy(
-            src_ref=spot,
-            dst_ref=spot,
-            send_sem=send_b.at[q, hop, j],
-            recv_sem=recv_b.at[q, hop, j],
-            device_id=torus.neighbour(other(axis), sign),
-            device_id_type=MESH,
-        )
-
-    for q in routes:
-        hop_a(q, 0).start()
-        hop_b(q, 0, 0).start()
-    for step in range(1, 2 * SIDE - 1):
-        for q in routes:
-            if step < SIDE:
-                hop_a(q, step - 1).wait_recv()
-                if step < SIDE - 1:
-                    hop_a(q, step).start()
-                hop_b(q, 0, step).start()
-        for q in routes:
-            for hop in range(SIDE - 1):
-                j = step - 1 - hop
-                if 0 <= j < SIDE:
-                    hop_b(q, hop, j).wait_recv()
-                    if hop < SIDE - 2:
-                        hop_b(q, hop + 1, j).start()
-    for q in routes:
-        for hop in range(SIDE - 1):
-            hop_a(q, hop).wait_send()
-            for j in range(SIDE):
-                hop_b(q, hop, j).wait_send()
-    sent = packed.at[pl.ds(0, devices - 1)]
-    pltpu.make_async_copy(sent, sent, out_sem).wait()
-
-
-def exchanged(pieces, slot, row, part, devices):
-    width = pieces.shape[1]
-    routes = len(ROUTES)
-    hops = SIDE - 1
-    part_rows = RD // routes
-    vmem = pl.BlockSpec(memory_space=pltpu.VMEM)
-    sems_a = pltpu.SemaphoreType.DMA((routes, hops))
-    sems_b = pltpu.SemaphoreType.DMA((routes, hops, SIDE))
-    return pl.pallas_call(
-        exchange_kernel,
-        out_shape=(
-            jax.ShapeDtypeStruct((RD, width), jnp.float32),
-            jax.ShapeDtypeStruct((SIDE, SIDE, routes, part_rows, width), jnp.bfloat16),
-        ),
-        in_specs=[vmem] * 4,
-        out_specs=(vmem, vmem),
-        scratch_shapes=[
-            pltpu.VMEM((devices, CAP, width), jnp.bfloat16),
-            pltpu.VMEM((devices, CAP, width), jnp.bfloat16),
-            pltpu.VMEM((2, RD, devices * CAP), jnp.bfloat16),
-            pltpu.SemaphoreType.DMA,
-            pltpu.SemaphoreType.DMA,
-            pltpu.SemaphoreType.DMA,
-            sems_a,
-            sems_a,
-            sems_b,
-            sems_b,
-        ],
-        compiler_params=pltpu.CompilerParams(
-            collective_id=1, has_side_effects=True, vmem_limit_bytes=32 * 1024 * 1024
-        ),
-        name="exchange_pieces",
-    )(pieces, slot, row, part)
+    )(particles, references, inv_noise, blocks.T, destination, row_index, fraction, slot)
 
 
 def send_slots(dests, devices):
@@ -602,16 +621,14 @@
     dom_pos = lax.axis_index("dom")
     slab_pos = lax.axis_index("slab")
     share = orients // dom_size
-    pieces, row, part = summed_slices(
-        particles, references, inv_noise, blocks, destination, row_index, fraction, dom_size, slab_size
-    )
-    pieces = pieces.reshape(groups * share, row_width)
-
     my_dest = lax.dynamic_slice(
         destination, (slab_pos * groups, dom_pos * share), (groups, share)
     )
     slot = send_slots(my_dest.reshape(-1), devices)
-    volume, next_slab = exchanged(pieces, slot[None, :], row, part, devices)
+    volume, next_slab = project(
+        particles, references, inv_noise, blocks, destination, row_index, fraction,
+        slot[None, :], dom_size, slab_size,
+    )
     next_slab = next_slab.reshape(dom_size * RD, row_width)
     return (volume, next_slab)
 

time: 151 us -> 141 us (0.934)
  Pallas kernels: 143 us -> 133 us
    pallas_call x2 -> x1, Pallas kernels: 143 us -> 133 us  [project(): pl.pallas_call(project_kernel, out_shape=(jax.ShapeDtypeStruct((RD, width...]
    unnamed x11 -> x2, local copies, waits for them, and re-layouts: 5.36 us -> 4.71 us
where the time goes in v6:
time: 141 us; the launch traced here: 140 us
  Pallas kernels  133 us (94%)
  local copies, waits for them, and re-layouts  4.87 us (3%)
  other arithmetic  1.42 us (1%)
    pallas_call x1, Pallas kernels, project(): pl.pallas_call(project_kernel, out_shape=(jax.ShapeDtypeStruct((RD, width...  133 us
    unnamed x2, local copies, waits for them, and re-layouts  4.71 us

profile of v6, /device:TPU:0, one launch (start us, length us, event | category | flops | bytes accessed | tf_op | source)
XLA Modules:
  0.0 140.4 jit_solution(7355366259597914753)
XLA Ops:
  0.6 0.8 broadcast_multiply_fusion
  1.4 0.1 mul.26
  1.5 0.1 eq.15
  1.6 0.9 fusion.2
  2.6 0.6 reshape_add_fusion.slot_ref
  3.2 132.5 %project.1 = (f32[256,256]{1,0:T(8,128)}, bf16[4,4,2,2,64,256]{5,4,3,2,1,0:T(8,128)(2,1)}) custom-call(bf16[512,40,256]{2,1,0:T(8,128)(2,1)} %x_ref.1, bf16[512,40,256]{2,1,0:T(8,128)(2,1)} %r_ref.1, f32[40]{0:T(128)} %noise_ref.1, s32[2,512]{1,0:T(2,128)} %bitcast.3, s32[320,512]{1,0:T(8,128)} %dest_ref.1, s32[320,512]{1,0:T(8,128)} %row_ref.1, ...), custom_call_target="tpu_custom_call" | custom-call | tf_op jit(solution)/shard_map/project/pallas_call | solution.py:543
  135.7 1.7 %copy.11 = f32[256,256]{1,0:T(8,128)} copy(f32[256,256]{1,0:T(8,128)} %get-tuple-element.10) | data formatting | bytes 524288
  137.4 3.0 %copy.12 = bf16[4096,256]{1,0:T(8,128)(2,1)} copy(bf16[4096,256]{1,0:T(8,128)(2,1)} %bitcast.2) | data formatting | bytes 4194304
  (1 shorter events, 0.0 us)

commit v7 on v6

--- a/solution.py
+++ b/solution.py
@@ -13,8 +13,9 @@
 CAP = 16
 SIDE = 4
 CHUNKS = 5
+VMEM_MIB = 56
 TILE = 8
-ROWS = 16
+ROWS = 32
 BAND = 256
 ROUTES = (("x", 1), ("x", -1), ("y", 1), ("y", -1))
 
@@ -35,7 +36,20 @@
     return "y" if axis == "x" else "x"
 
 
-def partial_scores(x_ref, r_ref, noise_ref, images, scores, raw_x, raw_r, weighted, x_sem, r_sem):
+def held(torus, q):
+    return lax.rem(torus.at[other(ROUTES[q][0])], 2)
+
+
+def partner(torus, q):
+    axis, sign = ROUTES[q]
+    return torus.neighbour(other(axis), sign * (1 - 2 * held(torus, q)))
+
+
+def group_of(q, i, which):
+    return (i * len(ROUTES) + q) * 2 + which
+
+
+def partial_scores(x_ref, r_ref, noise_ref, images, scores, begin, ready, raw_x, raw_r, weighted, x_sem, r_sem):
     particles, groups, _ = x_ref.shape
     orients = r_ref.shape[0]
     tile = raw_x.shape[2]
@@ -53,6 +67,7 @@
 
     start(0)
     start(1)
+    begin()
     scores[...] = jnp.zeros_like(scores)
 
     @pl.loop(0, tiles)
@@ -79,6 +94,8 @@
         @pl.when(t + 2 < tiles)
         def _():
             start(t + 2)
+
+        ready(t)
 
         for m in range(0, particles, BAND):
             acc = scores[m : m + BAND]
@@ -139,6 +156,16 @@
     row_out[...] = row_out[...] - 1.0
 
 
+def spread(compact, blocks, post_ref):
+    values = compact[...].astype(jnp.float32)
+    half = blocks.shape[0] // 2
+    first, second = blocks[0:1], blocks[half : half + 1]
+    for b in range(post_ref.shape[0] // OB):
+        value = jnp.where(first == b, values[:OB], 0.0)
+        value = jnp.where(second == b, values[OB:], value)
+        post_ref[b * OB : (b + 1) * OB] = value.astype(jnp.bfloat16)
+
+
 class Column:
     def __init__(self):
         self.dom = lax.axis_index("dom")
@@ -154,7 +181,7 @@
 
 
 def posteriors(
-    column, scores_ref, chosen_ref, post_ref, meanwhile, afterwards,
+    column, scores_ref, chosen_ref, own_blocks, compact, post_ref, meanwhile, afterwards, done,
     mine, from_mate, total, from_chips, found,
     mate_send, mate_recv, chip_send, chip_recv, back_send, back_recv, last_send, last_recv,
 ):
@@ -232,11 +259,9 @@
     last.start()
     last.wait_recv()
     everyone = found[...].astype(jnp.float32).reshape(slabs * count, 2 * OB)
-    first, second = chosen_ref[:, 0:1], chosen_ref[:, SIDE : SIDE + 1]
-    for b in range(scores_ref.shape[1] // OB):
-        value = jnp.where(first == b, everyone[:, :OB], 0.0)
-        value = jnp.where(second == b, everyone[:, OB:], value)
-        post_ref[b * OB : (b + 1) * OB, :] = value.T.astype(jnp.bfloat16)
+    compact[...] = everyone.T.astype(jnp.bfloat16)
+    done()
+    spread(compact, own_blocks, post_ref)
     to_mate.wait_send()
     last.wait_send()
     for step in range(1, chips):
@@ -244,21 +269,18 @@
         back(step).wait_send()
 
 
-def sum_over_dom(torus, images, post_ref, out_ref, partial, got1, got2, send1, recv1, send2, recv2):
-    per_chunk = images.shape[0] // (len(ROUTES) * CHUNKS)
+def sum_over_dom(
+    torus, images, post_ref, swapped, other_post, other_ready, swap, out_ref,
+    partial, got1, got2, send1, recv1, send2, recv2,
+):
     share = out_ref.shape[1]
-
-    def first_group(q, i):
-        return (i * len(ROUTES) + q) * per_chunk
-
-    def block(q, stage, hop):
-        axis, sign = ROUTES[q]
-        axis = axis if stage == 1 else other(axis)
-        return lax.rem(torus.at[axis] - sign * (1 + hop) + 2 * SIDE, SIDE)
+    last = SIDE - 2
+    steps = (1, -1, 2)
 
     def hop1(q, hop, i):
         axis, sign = ROUTES[q]
-        source = partial.at[q, i, block(q, 1, 0)] if hop == 0 else got1.at[q, hop - 1, i]
+        block = lax.rem(torus.at[axis] - sign + SIDE, SIDE)
+        source = partial.at[q, i, block] if hop == 0 else got1.at[q, hop - 1, i]
         return pltpu.make_async_remote_copy(
             src_ref=source,
             dst_ref=got1.at[q, hop, i],
@@ -268,15 +290,15 @@
             device_id_type=MESH,
         )
 
-    def hop2(q, hop, i):
-        axis, sign = ROUTES[q]
-        source = got1.at[q, SIDE - 2, i, block(q, 2, 0)] if hop == 0 else got2.at[q, hop - 1, i]
+    def hop2(q, k, i):
+        axis = other(ROUTES[q][0])
+        block = lax.rem(torus.at[axis] + steps[k] + SIDE, SIDE)
         return pltpu.make_async_remote_copy(
-            src_ref=source,
-            dst_ref=got2.at[q, hop, i],
-            send_sem=send2.at[q, hop, i],
-            recv_sem=recv2.at[q, hop, i],
-            device_id=torus.neighbour(other(axis), sign),
+            src_ref=got1.at[q, last, i, block],
+            dst_ref=got2.at[q, k, i],
+            send_sem=send2.at[q, k, i],
+            recv_sem=recv2.at[q, k, i],
+            device_id=torus.neighbour(axis, steps[k]),
             device_id_type=MESH,
         )
 
@@ -284,58 +306,54 @@
         return (a.astype(jnp.float32) + b.astype(jnp.float32)).astype(jnp.bfloat16)
 
     routes = range(len(ROUTES))
+    for q in routes:
+        other_ready(q)
 
     @pl.loop(0, CHUNKS)
     def _(i):
         for q in routes:
-            for j in range(per_chunk):
-                value = jnp.dot(
-                    post_ref[...], images[first_group(q, i) + j], preferred_element_type=jnp.float32
-                ).astype(jnp.bfloat16)
-                for yy in range(SIDE):
-                    for xx in range(SIDE):
-                        first, second = (xx, yy) if ROUTES[q][0] == "x" else (yy, xx)
-                        begin = (yy * SIDE + xx) * share
-                        partial[q, i, first, second, j] = value[begin : begin + share]
+            swap(q, i).wait_recv()
+            value = jnp.dot(
+                post_ref[...], images[group_of(q, i, held(torus, q))], preferred_element_type=jnp.float32
+            )
+            value = value + jnp.dot(other_post[q], swapped[q, i], preferred_element_type=jnp.float32)
+            value = value.astype(jnp.bfloat16)
+            for yy in range(SIDE):
+                for xx in range(SIDE):
+                    first, second = (xx, yy) if ROUTES[q][0] == "x" else (yy, xx)
+                    begin = (yy * SIDE + xx) * share
+                    partial[q, i, first, second] = value[begin : begin + share]
             hop1(q, 0, i).start()
 
-    for hop in range(SIDE - 2):
+    for hop in range(SIDE - 1):
 
         @pl.loop(0, CHUNKS)
         def _(i):
             for q in routes:
+                axis, sign = ROUTES[q]
+                block = lax.rem(torus.at[axis] - sign * (2 + hop) + 2 * SIDE, SIDE)
                 hop1(q, hop, i).wait_recv()
-                got1[q, hop, i] = added(got1[q, hop, i], partial[q, i, block(q, 1, hop + 1)])
-                hop1(q, hop + 1, i).start()
-
-    last = SIDE - 2
+                got1[q, hop, i] = added(got1[q, hop, i], partial[q, i, block])
+                if hop < last:
+                    hop1(q, hop + 1, i).start()
+                else:
+                    for k in range(len(steps)):
+                        hop2(q, k, i).start()
 
     @pl.loop(0, CHUNKS)
     def _(i):
         for q in routes:
-            hop1(q, last, i).wait_recv()
-            got1[q, last, i] = added(got1[q, last, i], partial[q, i, torus.at[ROUTES[q][0]]])
-            hop2(q, 0, i).start()
-
-    for hop in range(SIDE - 2):
-
-        @pl.loop(0, CHUNKS)
-        def _(i):
-            for q in routes:
-                hop2(q, hop, i).wait_recv()
-                got2[q, hop, i] = added(got2[q, hop, i], got1[q, last, i, block(q, 2, hop + 1)])
-                hop2(q, hop + 1, i).start()
+            for k in range(len(steps)):
+                hop2(q, k, i).wait_recv()
+            kept = held(torus, q)
+            mine = got1[q, last, i, torus.at[other(ROUTES[q][0])]]
+            out_ref[group_of(q, i, kept)] = added(got2[q, 2, i], mine)
+            out_ref[group_of(q, i, 1 - kept)] = added(got2[q, 0, i], got2[q, 1, i])
 
     @pl.loop(0, CHUNKS)
     def _(i):
         for q in routes:
-            hop2(q, last, i).wait_recv()
-            mine = got1[q, last, i, torus.at[other(ROUTES[q][0])]]
-            out_ref[pl.ds(first_group(q, i), per_chunk)] = added(got2[q, last, i], mine)
-
-    @pl.loop(0, CHUNKS)
-    def _(i):
-        for q in routes:
+            swap(q, i).wait_send()
             for hop in range(SIDE - 1):
                 hop1(q, hop, i).wait_send()
                 hop2(q, hop, i).wait_send()
@@ -489,7 +507,9 @@
 def project_kernel(
     x_ref, r_ref, noise_ref, blocks_ref, dest_ref, row_ref, part_ref, slot_ref,
     volume_ref, next_ref,
-    images, scores, raw_x, raw_r, weighted, post, chosen, row_at, part_at, insert, pieces, *rest
+    images, scores, raw_x, raw_r, weighted, post, chosen, row_at, part_at, insert, pieces,
+    swapped, own_blocks, other_blocks, compact, other_compact, other_post,
+    swap_send, swap_recv, block_send, block_recv, compact_send, compact_recv, *rest
 ):
     x_sem, r_sem = rest[:2]
     post_scratch = rest[2:7]
@@ -509,9 +529,51 @@
     both = blocks_ref[...].astype(jnp.float32)
     half = chosen.shape[1] // 2
     both = jnp.concatenate([both[0:1]] * half + [both[1:2]] * half, axis=0)
+    own_blocks[...] = both
     chosen[...] = both.T
-    partial_scores(x_ref, r_ref, noise_ref, images, scores, raw_x, raw_r, weighted, x_sem, r_sem)
-    pl.semaphore_wait(barrier, len(others))
+    routes = range(len(ROUTES))
+
+    def to_partner(q, source, target, send, recv):
+        return pltpu.make_async_remote_copy(
+            src_ref=source,
+            dst_ref=target,
+            send_sem=send,
+            recv_sem=recv,
+            device_id=partner(torus, q),
+            device_id_type=MESH,
+        )
+
+    def swap(q, i):
+        away = images.at[group_of(q, i, 1 - held(torus, q))]
+        return to_partner(q, away, swapped.at[q, i], swap_send.at[q, i], swap_recv.at[q, i])
+
+    def share_blocks(q):
+        return to_partner(q, own_blocks, other_blocks.at[q], block_send.at[q], block_recv.at[q])
+
+    def share_post(q):
+        return to_partner(q, compact, other_compact.at[q], compact_send.at[q], compact_recv.at[q])
+
+    def begin():
+        pl.semaphore_wait(barrier, len(others))
+        for q in routes:
+            share_blocks(q).start()
+
+    def ready(t):
+        for q in routes:
+            swap(q, t).start()
+
+    def done():
+        for q in routes:
+            share_post(q).start()
+
+    def other_ready(q):
+        share_blocks(q).wait_recv()
+        share_post(q).wait_recv()
+        spread(other_compact.at[q], other_blocks.at[q], other_post.at[q])
+
+    partial_scores(
+        x_ref, r_ref, noise_ref, images, scores, begin, ready, raw_x, raw_r, weighted, x_sem, r_sem
+    )
 
     def tables():
         slot_tables(dest_ref, row_ref, part_ref, me, counts, rows_at, parts_at, row_at, part_at)
@@ -519,11 +581,17 @@
     def weights():
         insertion_weights(row_at, part_at, insert)
 
-    posteriors(column, scores, chosen, post, tables, weights, *post_scratch, *post_sems)
-    sum_over_dom(torus, images, post, pieces, *sum_scratch)
+    posteriors(
+        column, scores, chosen, own_blocks, compact, post, tables, weights, done,
+        *post_scratch, *post_sems,
+    )
+    sum_over_dom(torus, images, post, swapped, other_post, other_ready, swap, pieces, *sum_scratch)
     sent = insert_pieces(torus, pieces, slot_ref, insert, volume_ref, *insert_scratch)
     gather_rows(torus, volume_ref, next_ref, *gather_sems)
     sent.wait()
+    for q in routes:
+        share_blocks(q).wait_send()
+        share_post(q).wait_send()
 
 
 def project(particles, references, inv_noise, blocks, destination, row_index, fraction, slot, doms, slabs):
@@ -535,7 +603,7 @@
     devices = doms * slabs
     routes = len(ROUTES)
     hops = SIDE - 1
-    piece = (groups // (routes * CHUNKS), share, width)
+    piece = (share, width)
     vmem = pl.BlockSpec(memory_space=pltpu.VMEM)
     hbm = pl.BlockSpec(memory_space=pl.ANY)
     dma = pltpu.SemaphoreType.DMA
@@ -560,6 +628,18 @@
             table,
             pltpu.VMEM((2, RD, devices * CAP), jnp.bfloat16),
             pltpu.VMEM((groups, share, width), jnp.bfloat16),
+            pltpu.VMEM((routes, CHUNKS, count, width), jnp.bfloat16),
+            pltpu.VMEM((8, count), jnp.float32),
+            pltpu.VMEM((routes, 8, count), jnp.float32),
+            pltpu.VMEM((2 * OB, count), jnp.bfloat16),
+            pltpu.VMEM((routes, 2 * OB, count), jnp.bfloat16),
+            pltpu.VMEM((routes, orients, count), jnp.bfloat16),
+            dma((routes, CHUNKS)),
+            dma((routes, CHUNKS)),
+            dma((routes,)),
+            dma((routes,)),
+            dma((routes,)),
+            dma((routes,)),
             dma((2,)),
             dma((2,)),
             pltpu.VMEM((2, chips, part, 2 * OB), jnp.float32),
@@ -596,7 +676,7 @@
             dma((2, 2, SIDE, 2)),
         ],
         compiler_params=pltpu.CompilerParams(
-            collective_id=0, has_side_effects=True, vmem_limit_bytes=60 * 1024 * 1024
+            collective_id=0, has_side_effects=True, vmem_limit_bytes=VMEM_MIB * 1024 * 1024
         ),
         name="project",
     )(particles, references, inv_noise, blocks.T, destination, row_index, fraction, slot)

time: 141 us -> 131 us (0.929)
  Pallas kernels: 133 us -> 123 us
    pallas_call x1, Pallas kernels: 133 us -> 123 us  [project(): pl.pallas_call(project_kernel, out_shape=(jax.ShapeDtypeStruct((RD, width...]
where the time goes in v7:
time: 131 us
  Pallas kernels  123 us (94%)
  local copies, waits for them, and re-layouts  4.87 us (4%)
  other arithmetic  1.42 us (1%)
    pallas_call x1, Pallas kernels, project(): pl.pallas_call(project_kernel, out_shape=(jax.ShapeDtypeStruct((RD, width...  123 us
    unnamed x2, local copies, waits for them, and re-layouts  4.71 us

profile of v7, /device:TPU:0, one launch (start us, length us, event | category | flops | bytes accessed | tf_op | source)
XLA Modules:
  0.0 130.8 jit_solution(1639052644374779854)
XLA Ops:
  0.6 0.8 broadcast_multiply_fusion
  1.4 0.1 mul.26
  1.5 0.1 eq.15
  1.6 0.9 fusion.2
  2.6 0.6 reshape_add_fusion.slot_ref
  3.2 122.9 %project.1 = (f32[256,256]{1,0:T(8,128)}, bf16[4,4,2,2,64,256]{5,4,3,2,1,0:T(8,128)(2,1)}) custom-call(bf16[512,40,256]{2,1,0:T(8,128)(2,1)} %x_ref.1, bf16[512,40,256]{2,1,0:T(8,128)(2,1)} %r_ref.1, f32[40]{0:T(128)} %noise_ref.1, s32[2,512]{1,0:T(2,128)} %bitcast.3, s32[320,512]{1,0:T(8,128)} %dest_ref.1, s32[320,512]{1,0:T(8,128)} %row_ref.1, ...), custom_call_target="tpu_custom_call" | custom-call | tf_op jit(solution)/shard_map/project/pallas_call | solution.py:611
  126.1 1.7 %copy.11 = f32[256,256]{1,0:T(8,128)} copy(f32[256,256]{1,0:T(8,128)} %get-tuple-element.10) | data formatting | bytes 524288
  127.7 3.0 %copy.12 = bf16[4096,256]{1,0:T(8,128)(2,1)} copy(bf16[4096,256]{1,0:T(8,128)(2,1)} %bitcast.2) | data formatting | bytes 4194304
  (1 shorter events, 0.0 us)

commit v8 on v7

--- a/solution.py
+++ b/solution.py
@@ -13,7 +13,8 @@
 CAP = 16
 SIDE = 4
 CHUNKS = 5
-VMEM_MIB = 56
+VMEM_MIB = 49
+LATE = 1
 TILE = 8
 ROWS = 32
 BAND = 256
@@ -157,12 +158,11 @@
 
 
 def spread(compact, blocks, post_ref):
-    values = compact[...].astype(jnp.float32)
     half = blocks.shape[0] // 2
     first, second = blocks[0:1], blocks[half : half + 1]
     for b in range(post_ref.shape[0] // OB):
-        value = jnp.where(first == b, values[:OB], 0.0)
-        value = jnp.where(second == b, values[OB:], value)
+        value = jnp.where(first == b, compact[0].astype(jnp.float32), 0.0)
+        value = jnp.where(second == b, compact[1].astype(jnp.float32), value)
         post_ref[b * OB : (b + 1) * OB] = value.astype(jnp.bfloat16)
 
 
@@ -259,7 +259,8 @@
     last.start()
     last.wait_recv()
     everyone = found[...].astype(jnp.float32).reshape(slabs * count, 2 * OB)
-    compact[...] = everyone.T.astype(jnp.bfloat16)
+    for which in range(2):
+        compact[which] = everyone[:, which * OB : (which + 1) * OB].T.astype(jnp.bfloat16)
     done()
     spread(compact, own_blocks, post_ref)
     to_mate.wait_send()
@@ -270,7 +271,7 @@
 
 
 def sum_over_dom(
-    torus, images, post_ref, swapped, other_post, other_ready, swap, out_ref,
+    torus, images, post_ref, swapped, other_post, others_ready, swap, out_ref,
     partial, got1, got2, send1, recv1, send2, recv2,
 ):
     share = out_ref.shape[1]
@@ -306,8 +307,7 @@
         return (a.astype(jnp.float32) + b.astype(jnp.float32)).astype(jnp.bfloat16)
 
     routes = range(len(ROUTES))
-    for q in routes:
-        other_ready(q)
+    others_ready()
 
     @pl.loop(0, CHUNKS)
     def _(i):
@@ -371,7 +371,7 @@
         insert[1, :, b * lanes : (b + 1) * lanes] = (weight - high.astype(jnp.float32)).astype(jnp.bfloat16)
 
 
-def insert_pieces(torus, pieces_ref, slot_ref, insert, volume_ref, packed, got, own_sem, out_sem, in_sem):
+def insert_pieces(torus, pieces_ref, slot_ref, insert, volume_ref, buffers, own_sem, out_sem, in_sem):
     slabs = lax.axis_size("slab")
     devices = lax.axis_size("dom") * slabs
     me = (torus.at["y"] * SIDE + torus.at["x"]) * slabs + torus.slab
@@ -380,6 +380,14 @@
     block = RD
     owners = block // CAP
     numbers = lax.broadcasted_iota(jnp.int32, (block, count), 0)
+    folds = CAP // TILE
+
+    def packed(first, number=1):
+        return buffers.at[0, pl.ds(first * folds, number * folds)]
+
+    def got(first, number=1):
+        return buffers.at[1, pl.ds(first * folds, number * folds)]
+
     pieces = pieces_ref[...].reshape(count, width)
 
     @pl.loop(0, devices // owners)
@@ -388,7 +396,8 @@
         first = b * owners
         pick = (numbers + b * block == slot_ref[...]).astype(jnp.float32).astype(jnp.bfloat16)
         value = jnp.dot(pick, pieces, preferred_element_type=jnp.float32)
-        packed[pl.ds(first, owners)] = value.astype(jnp.bfloat16).reshape(owners, CAP, width)
+        value = value.astype(jnp.bfloat16).reshape(owners * folds, TILE, width)
+        buffers[0, pl.ds(first * folds, owners * folds)] = value
 
         @pl.loop(0, owners)
         def _(j):
@@ -397,23 +406,23 @@
             @pl.when(to != me)
             def _():
                 pltpu.make_async_remote_copy(
-                    src_ref=packed.at[to],
-                    dst_ref=got.at[me],
+                    src_ref=packed(to),
+                    dst_ref=got(me),
                     send_sem=out_sem,
                     recv_sem=in_sem,
                     device_id=(lax.div(to, slabs), lax.rem(to, slabs)),
                     device_id_type=MESH,
                 ).start()
 
-    own = pltpu.make_async_copy(packed.at[me], got.at[me], own_sem)
+    own = pltpu.make_async_copy(packed(me), got(me), own_sem)
     own.start()
     own.wait()
-    others = got.at[pl.ds(0, devices - 1)]
+    others = got(0, devices - 1)
     pltpu.make_async_copy(others, others, in_sem).wait()
-    received = got[...].reshape(devices * CAP, width)
+    received = buffers[1, 0 : devices * folds].reshape(devices * CAP, width)
     volume = jnp.dot(insert[0], received, preferred_element_type=jnp.float32)
     volume_ref[...] = volume + jnp.dot(insert[1], received, preferred_element_type=jnp.float32)
-    sent = packed.at[pl.ds(0, devices - 1)]
+    sent = packed(0, devices - 1)
     return pltpu.make_async_copy(sent, sent, out_sem)
 
 
@@ -509,15 +518,16 @@
     volume_ref, next_ref,
     images, scores, raw_x, raw_r, weighted, post, chosen, row_at, part_at, insert, pieces,
     swapped, own_blocks, other_blocks, compact, other_compact, other_post,
-    swap_send, swap_recv, block_send, block_recv, compact_send, compact_recv, *rest
+    swap_send, swap_recv, block_send, block_recv, compact_send, compact_recv, pass_send, pass_recv,
+    *rest
 ):
     x_sem, r_sem = rest[:2]
     post_scratch = rest[2:7]
     counts, rows_at, parts_at = rest[7:10]
     post_sems = rest[10:18]
     sum_scratch = rest[18:25]
-    insert_scratch = rest[25:30]
-    gather_sems = rest[30:]
+    insert_sems = rest[25:28]
+    gather_sems = rest[28:]
     torus = Torus()
     column = Column()
     me = column.dom * column.slabs + column.slab
@@ -550,8 +560,22 @@
     def share_blocks(q):
         return to_partner(q, own_blocks, other_blocks.at[q], block_send.at[q], block_recv.at[q])
 
+    core = column.core
+
     def share_post(q):
-        return to_partner(q, compact, other_compact.at[q], compact_send.at[q], compact_recv.at[q])
+        target = other_compact.at[q, core]
+        return to_partner(q, compact.at[core], target, compact_send.at[q], compact_recv.at[q])
+
+    def pass_post(q):
+        half_of = other_compact.at[q, core]
+        return pltpu.make_async_remote_copy(
+            src_ref=half_of,
+            dst_ref=half_of,
+            send_sem=pass_send.at[q],
+            recv_sem=pass_recv.at[q],
+            device_id=column.mate,
+            device_id_type=MESH,
+        )
 
     def begin():
         pl.semaphore_wait(barrier, len(others))
@@ -559,17 +583,26 @@
             share_blocks(q).start()
 
     def ready(t):
-        for q in routes:
-            swap(q, t).start()
+        @pl.when(t < CHUNKS - LATE)
+        def _():
+            for q in routes:
+                swap(q, t).start()
 
     def done():
         for q in routes:
             share_post(q).start()
-
-    def other_ready(q):
-        share_blocks(q).wait_recv()
-        share_post(q).wait_recv()
-        spread(other_compact.at[q], other_blocks.at[q], other_post.at[q])
+        for i in range(CHUNKS - LATE, CHUNKS):
+            for q in routes:
+                swap(q, i).start()
+
+    def others_ready():
+        for q in routes:
+            share_post(q).wait_recv()
+            pass_post(q).start()
+        for q in routes:
+            share_blocks(q).wait_recv()
+            pass_post(q).wait_recv()
+            spread(other_compact.at[q], other_blocks.at[q], other_post.at[q])
 
     partial_scores(
         x_ref, r_ref, noise_ref, images, scores, begin, ready, raw_x, raw_r, weighted, x_sem, r_sem
@@ -585,13 +618,14 @@
         column, scores, chosen, own_blocks, compact, post, tables, weights, done,
         *post_scratch, *post_sems,
     )
-    sum_over_dom(torus, images, post, swapped, other_post, other_ready, swap, pieces, *sum_scratch)
-    sent = insert_pieces(torus, pieces, slot_ref, insert, volume_ref, *insert_scratch)
+    sum_over_dom(torus, images, post, swapped, other_post, others_ready, swap, pieces, *sum_scratch)
+    sent = insert_pieces(torus, pieces, slot_ref, insert, volume_ref, raw_x, *insert_sems)
     gather_rows(torus, volume_ref, next_ref, *gather_sems)
     sent.wait()
     for q in routes:
         share_blocks(q).wait_send()
         share_post(q).wait_send()
+        pass_post(q).wait_send()
 
 
 def project(particles, references, inv_noise, blocks, destination, row_index, fraction, slot, doms, slabs):
@@ -631,11 +665,13 @@
             pltpu.VMEM((routes, CHUNKS, count, width), jnp.bfloat16),
             pltpu.VMEM((8, count), jnp.float32),
             pltpu.VMEM((routes, 8, count), jnp.float32),
-            pltpu.VMEM((2 * OB, count), jnp.bfloat16),
-            pltpu.VMEM((routes, 2 * OB, count), jnp.bfloat16),
+            pltpu.VMEM((2, OB, count), jnp.bfloat16),
+            pltpu.VMEM((routes, 2, OB, count), jnp.bfloat16),
             pltpu.VMEM((routes, orients, count), jnp.bfloat16),
             dma((routes, CHUNKS)),
             dma((routes, CHUNKS)),
+            dma((routes,)),
+            dma((routes,)),
             dma((routes,)),
             dma((routes,)),
             dma((routes,)),
@@ -665,8 +701,6 @@
             dma((routes, hops, CHUNKS)),
             dma((routes, hops, CHUNKS)),
             dma((routes, hops, CHUNKS)),
-            pltpu.VMEM((devices, CAP, width), jnp.bfloat16),
-            pltpu.VMEM((devices, CAP, width), jnp.bfloat16),
             dma,
             dma,
             dma,

time: 131 us -> 124 us (0.947)
  Pallas kernels: 123 us -> 119 us
  local copies, waits for them, and re-layouts: 4.87 us -> 2.2 us
    pallas_call x1, Pallas kernels: 123 us -> 119 us  [project(): pl.pallas_call(project_kernel, out_shape=(jax.ShapeDtypeStruct((RD, width...]
    unnamed x2 -> x12, local copies, waits for them, and re-layouts: 4.71 us -> 2.04 us
where the time goes in v8:
time: 124 us; the launch traced here: 123 us
  Pallas kernels  119 us (96%)
  local copies, waits for them, and re-layouts  2.2 us (2%)
    pallas_call x1, Pallas kernels, project(): pl.pallas_call(project_kernel, out_shape=(jax.ShapeDtypeStruct((RD, width...  119 us

profile of v8, /device:TPU:0, one launch (start us, length us, event | category | flops | bytes accessed | tf_op | source)
XLA Modules:
  0.0 123.4 jit_solution(12448050288083175215)
XLA Ops:
  0.6 0.0 copy-start
  0.6 0.0 copy-start.2
  0.7 0.0 copy-start.1
  0.7 0.0 copy-start.4
  0.7 0.0 copy-start.3
  0.7 0.9 broadcast_multiply_fusion
  1.6 0.1 mul.26
  1.7 0.1 eq.15
  1.8 0.9 fusion.2
  2.7 0.0 copy-done
  2.8 0.0 copy-done.2
  2.8 0.0 copy-done.1
  2.8 0.0 copy-done.4
  2.8 0.0 copy-done.3
  2.8 118.6 %project.1 = (f32[256,256]{1,0:T(8,128)S(1)}, bf16[4,4,2,2,64,256]{5,4,3,2,1,0:T(8,128)(2,1)S(1)}) custom-call(bf16[512,40,256]{2,1,0:T(8,128)(2,1)} %x_ref.1, bf16[512,40,256]{2,1,0:T(8,128)(2,1)} %r_ref.1, f32[40]{0:T(128)S(1)} %copy-done.4, s32[2,512]{1,0:T(2,128)S(1)} %bitcast.3, s32[320,512]{1,0:T(8,128)S(1)} %copy-done, s32[320,512]{1,0:T(8,128)S(1)} %copy-done.1, ...), custom_call_target="tpu_custom_call" | custom-call | tf_op jit(solution)/shard_map/project/pallas_call | solution.py:645
  121.4 0.7 copy.11
  122.1 1.3 %copy.12 = bf16[4096,256]{1,0:T(8,128)(2,1)} copy(bf16[4096,256]{1,0:T(8,128)(2,1)S(1)} %bitcast.2) | data formatting | bytes 4194304
  (2 shorter events, 0.0 us)
Async XLA Ops:
  0.6 2.1 %copy-start = (s32[320,512]{1,0:T(8,128)S(1)}, s32[320,512]{1,0:T(8,128)}, u32[]{:S(2)}) copy-start(s32[320,512]{1,0:T(8,128)} %dest_ref.1) | copy-start | bytes 1966084
  0.6 2.1 %copy-start.2 = (f32[320,512]{1,0:T(8,128)S(1)}, f32[320,512]{1,0:T(8,128)}, u32[]{:S(2)}) copy-start(f32[320,512]{1,0:T(8,128)} %part_ref.1) | copy-start | bytes 1966084
  0.7 2.1 %copy-start.1 = (s32[320,512]{1,0:T(8,128)S(1)}, s32[320,512]{1,0:T(8,128)}, u32[]{:S(2)}) copy-start(s32[320,512]{1,0:T(8,128)} %row_ref.1) | copy-start | bytes 1966084
  0.7 2.1 %copy-start.4 = (f32[40]{0:T(128)S(1)}, f32[40]{0:T(128)}, u32[]{:S(2)}) copy-start(f32[40]{0:T(128)} %noise_ref.1) | copy-start | bytes 484
  0.7 2.1 %copy-start.3 = (s32[512,2]{0,1:T(2,128)S(1)}, s32[512,2]{0,1:T(2,128)}, u32[]{:S(2)}) copy-start(s32[512,2]{0,1:T(2,128)} %param.8) | copy-start | bytes 12292

commit v9 on v8

--- a/solution.py
+++ b/solution.py
@@ -14,9 +14,9 @@
 SIDE = 4
 CHUNKS = 5
 VMEM_MIB = 49
-LATE = 1
+LATE = 2
 TILE = 8
-ROWS = 32
+ROWS = 64
 BAND = 256
 ROUTES = (("x", 1), ("x", -1), ("y", 1), ("y", -1))
 
@@ -181,7 +181,7 @@
 
 
 def posteriors(
-    column, scores_ref, chosen_ref, own_blocks, compact, post_ref, meanwhile, afterwards, done,
+    column, scores_ref, chosen_ref, own_blocks, compact, post_ref, done,
     mine, from_mate, total, from_chips, found,
     mate_send, mate_recv, chip_send, chip_recv, back_send, back_recv, last_send, last_recv,
 ):
@@ -224,7 +224,6 @@
 
     for step in range(1, chips):
         to_chip(step).start()
-    meanwhile()
     for step in range(1, chips):
         to_chip(step).wait_recv()
     scores = total[chip]
@@ -245,7 +244,6 @@
 
     for step in range(1, chips):
         back(step).start()
-    afterwards()
     for step in range(1, chips):
         back(step).wait_recv()
     last = pltpu.make_async_remote_copy(
@@ -271,7 +269,7 @@
 
 
 def sum_over_dom(
-    torus, images, post_ref, swapped, other_post, others_ready, swap, out_ref,
+    torus, images, post_ref, swapped, other_post, others_ready, swap, meanwhile, out_ref,
     partial, got1, got2, send1, recv1, send2, recv2,
 ):
     share = out_ref.shape[1]
@@ -340,6 +338,9 @@
                     for k in range(len(steps)):
                         hop2(q, k, i).start()
 
+        if hop < last:
+            meanwhile[hop]()
+
     @pl.loop(0, CHUNKS)
     def _(i):
         for q in routes:
@@ -380,6 +381,8 @@
     block = RD
     owners = block // CAP
     numbers = lax.broadcasted_iota(jnp.int32, (block, count), 0)
+    shift = CAP.bit_length() - 1
+    numbers = lax.shift_right_logical(numbers, shift) * (slabs * CAP) + (numbers & (CAP - 1))
     folds = CAP // TILE
 
     def packed(first, number=1):
@@ -390,18 +393,18 @@
 
     pieces = pieces_ref[...].reshape(count, width)
 
-    @pl.loop(0, devices // owners)
+    @pl.loop(0, slabs)
     def _(k):
-        b = lax.rem(lax.div(me, owners) + k, devices // owners)
-        first = b * owners
-        pick = (numbers + b * block == slot_ref[...]).astype(jnp.float32).astype(jnp.bfloat16)
+        b = lax.rem(torus.slab + k, slabs)
+        pick = (numbers + b * CAP == slot_ref[...]).astype(jnp.float32).astype(jnp.bfloat16)
         value = jnp.dot(pick, pieces, preferred_element_type=jnp.float32)
         value = value.astype(jnp.bfloat16).reshape(owners * folds, TILE, width)
-        buffers[0, pl.ds(first * folds, owners * folds)] = value
+        for j in range(owners):
+            buffers[0, pl.ds((j * slabs + b) * folds, folds)] = value[j * folds : (j + 1) * folds]
 
         @pl.loop(0, owners)
         def _(j):
-            to = first + lax.rem(me + j, owners)
+            to = lax.rem(lax.div(me, slabs) + j, owners) * slabs + b
 
             @pl.when(to != me)
             def _():
@@ -615,10 +618,10 @@
         insertion_weights(row_at, part_at, insert)
 
     posteriors(
-        column, scores, chosen, own_blocks, compact, post, tables, weights, done,
+        column, scores, chosen, own_blocks, compact, post, done,
         *post_scratch, *post_sems,
     )
-    sum_over_dom(torus, images, post, swapped, other_post, others_ready, swap, pieces, *sum_scratch)
+    sum_over_dom(torus, images, post, swapped, other_post, others_ready, swap, (tables, weights), pieces, *sum_scratch)
     sent = insert_pieces(torus, pieces, slot_ref, insert, volume_ref, raw_x, *insert_sems)
     gather_rows(torus, volume_ref, next_ref, *gather_sems)
     sent.wait()

time: 124 us -> 122 us (0.984); the launches traced: 123 us -> 120 us
  Pallas kernels: 119 us -> 115 us
    pallas_call x1, Pallas kernels: 119 us -> 115 us  [project(): pl.pallas_call(project_kernel, out_shape=(jax.ShapeDtypeStruct((RD, width...]
where the time goes in v9:
time: 122 us; the launch traced here: 120 us
  Pallas kernels  115 us (94%)
  local copies, waits for them, and re-layouts  2.2 us (2%)
    pallas_call x1, Pallas kernels, project(): pl.pallas_call(project_kernel, out_shape=(jax.ShapeDtypeStruct((RD, width...  115 us

profile of v9, /device:TPU:0, one launch (start us, length us, event | category | flops | bytes accessed | tf_op | source)
XLA Modules:
  0.0 119.7 jit_solution(7133060555369351775)
XLA Ops:
  0.6 0.0 copy-start
  0.6 0.0 copy-start.2
  0.7 0.0 copy-start.1
  0.7 0.0 copy-start.4
  0.7 0.0 copy-start.3
  0.7 0.9 broadcast_multiply_fusion
  1.6 0.1 mul.26
  1.7 0.1 eq.15
  1.8 0.9 fusion.2
  2.7 0.0 copy-done
  2.8 0.0 copy-done.2
  2.8 0.0 copy-done.1
  2.8 0.0 copy-done.4
  2.8 0.0 copy-done.3
  2.8 114.9 %project.1 = (f32[256,256]{1,0:T(8,128)S(1)}, bf16[4,4,2,2,64,256]{5,4,3,2,1,0:T(8,128)(2,1)S(1)}) custom-call(bf16[512,40,256]{2,1,0:T(8,128)(2,1)} %x_ref.1, bf16[512,40,256]{2,1,0:T(8,128)(2,1)} %r_ref.1, f32[40]{0:T(128)S(1)} %copy-done.4, s32[2,512]{1,0:T(2,128)S(1)} %bitcast.3, s32[320,512]{1,0:T(8,128)S(1)} %copy-done, s32[320,512]{1,0:T(8,128)S(1)} %copy-done.1, ...), custom_call_target="tpu_custom_call" | custom-call | tf_op jit(solution)/shard_map/project/pallas_call | solution.py:648
  117.7 0.7 copy.11
  118.4 1.3 %copy.12 = bf16[4096,256]{1,0:T(8,128)(2,1)} copy(bf16[4096,256]{1,0:T(8,128)(2,1)S(1)} %bitcast.2) | data formatting | bytes 4194304
  (2 shorter events, 0.0 us)
Async XLA Ops:
  0.6 2.1 %copy-start = (s32[320,512]{1,0:T(8,128)S(1)}, s32[320,512]{1,0:T(8,128)}, u32[]{:S(2)}) copy-start(s32[320,512]{1,0:T(8,128)} %dest_ref.1) | copy-start | bytes 1966084
  0.6 2.1 %copy-start.2 = (f32[320,512]{1,0:T(8,128)S(1)}, f32[320,512]{1,0:T(8,128)}, u32[]{:S(2)}) copy-start(f32[320,512]{1,0:T(8,128)} %part_ref.1) | copy-start | bytes 1966084
  0.7 2.1 %copy-start.1 = (s32[320,512]{1,0:T(8,128)S(1)}, s32[320,512]{1,0:T(8,128)}, u32[]{:S(2)}) copy-start(s32[320,512]{1,0:T(8,128)} %row_ref.1) | copy-start | bytes 1966084
  0.7 2.1 %copy-start.4 = (f32[40]{0:T(128)S(1)}, f32[40]{0:T(128)}, u32[]{:S(2)}) copy-start(f32[40]{0:T(128)} %noise_ref.1) | copy-start | bytes 484
  0.7 2.1 %copy-start.3 = (s32[512,2]{0,1:T(2,128)S(1)}, s32[512,2]{0,1:T(2,128)}, u32[]{:S(2)}) copy-start(s32[512,2]{0,1:T(2,128)} %param.8) | copy-start | bytes 12292
